TPU v7x, 768 devices: a whole 4x8x12 slice. The times are simulated.
768 devices in a mesh: slab: 48 (over x_lo, z, core), filt: 16 (over x_hi, y).
Axes of the slice: x: 4 (x_hi: 2, x_lo: 2; x = x_hi * 2 + x_lo), y: 8, z: 12, core: 2. Of those that a mesh axis runs over, the one named last changes fastest.
Arguments:
- volume: bfloat16 [2, 64, 192, 8, 256], P(None, 'filt', 'slab'), may hold values from -6 to 6
- first_weight: bfloat16 [64, 128, 2, 2, 2], P(None, 'filt'), may hold values from -0.25 to 0.25
- second_weight: bfloat16 [128, 128, 3, 3, 3], P(None, 'filt'), may hold values from -0.109375 to 0.109375
- out_grad: bfloat16 [2, 128, 96, 4, 128], P(None, 'filt', 'slab'), may hold values from -0.01953125 to 0.01953125
Outputs:
- result: bfloat16 [2, 128, 96, 4, 128], P(None, 'filt', 'slab')
- weight_one: float32 [64, 128, 2, 2, 2], P(None, 'filt')
- weight_two: float32 [128, 128, 3, 3, 3], P(None, 'filt')
All inputs are finite; a program needn't handle non-finite values.
Results may differ from a plain program's by a relative error of at most 0.0054.
Values may be sent and summed in bfloat16 or wider, within the bound.
A program may use at most 64 MiB of HBM per device.

v0:
```python
import jax
import jax.numpy as jnp
from jax import lax
from jax.sharding import PartitionSpec as P


def padded(array, sides, width):
    for axis, dim in sides:
        peers, length = (lax.axis_size(axis), array.shape[dim])
        up = [(i, (i + 1) % peers) for i in range(peers - 1)]
        down = [(j, i) for i, j in up]
        last = lax.slice_in_dim(array, length - width, length, axis=dim)
        leading = lax.slice_in_dim(array, 0, width, axis=dim)
        before = lax.ppermute(last, axis, up)
        after = lax.ppermute(leading, axis, down)
        array = jnp.concatenate([before, array, after], axis=dim)
    return array


def silu_value(values):
    return values * jax.nn.sigmoid(values)


def silu_slope(values):
    logistic = jax.nn.sigmoid(values)
    return logistic * (1.0 + values * (1.0 - logistic))


def pad_sides(values):
    return jnp.pad(values, ((0, 0), (0, 0), (0, 0), (1, 1), (1, 1)))


def first_conv(inputs, kernel):
    return lax.conv_general_dilated(
        inputs,
        kernel,
        (2, 2, 2),
        "VALID",
        dimension_numbers=("NCDHW", "IODHW", "NCDHW"),
        preferred_element_type=jnp.float32,
    )


def back_conv(grad_pad, kernel):
    return lax.conv_general_dilated(
        grad_pad,
        kernel[:, :, ::-1, ::-1, ::-1],
        (1, 1, 1),
        "VALID",
        dimension_numbers=("NCDHW", "OIDHW", "NCDHW"),
        preferred_element_type=jnp.float32,
    )


def on_device(volume, first_weight, second_weight, out_grad):
    extended = padded(volume, (("slab", 2),), 2)
    all_inputs = lax.all_gather(extended, "filt", axis=1, tiled=True)
    pre_own = first_conv(all_inputs, first_weight)
    own_hidden = silu_value(pre_own).astype(jnp.bfloat16)
    hidden_ext = lax.all_gather(own_hidden, "filt", axis=1, tiled=True)
    pre_own = pre_own[:, :, 1:-1]
    hidden_pad = pad_sides(hidden_ext)
    second_pre = lax.conv_general_dilated(
        hidden_pad,
        second_weight,
        (1, 1, 1),
        "VALID",
        dimension_numbers=("NCDHW", "IODHW", "NCDHW"),
        preferred_element_type=jnp.float32,
    )
    result = silu_value(second_pre).astype(jnp.bfloat16)
    second_grad = (out_grad.astype(jnp.float32) * silu_slope(second_pre)).astype(jnp.bfloat16)
    grad_ext = padded(second_grad, (("slab", 2),), 1)
    partial_grad = back_conv(pad_sides(grad_ext), second_weight)
    mid_grad = lax.psum_scatter(partial_grad, "filt", scatter_dimension=1, tiled=True)
    first_grad = (mid_grad * silu_slope(pre_own)).astype(jnp.bfloat16)
    weight_two = lax.conv_general_dilated(
        hidden_pad,
        second_grad,
        (1, 1, 1),
        "VALID",
        dimension_numbers=("CNDHW", "IODHW", "NCDHW"),
        preferred_element_type=jnp.float32,
    )
    own_inputs = all_inputs[:, :, 2:-2]
    weight_one = lax.conv_general_dilated(
        own_inputs,
        first_grad,
        (1, 1, 1),
        "VALID",
        rhs_dilation=(2, 2, 2),
        dimension_numbers=("CNDHW", "IODHW", "NCDHW"),
        preferred_element_type=jnp.float32,
    )
    weight_one, weight_two = lax.psum((weight_one, weight_two), "slab")
    return (result, weight_one, weight_two)


def solution(mesh):
    in_specs = (
        P(None, "filt", "slab", None, None),
        P(None, "filt", None, None, None),
        P(None, "filt", None, None, None),
        P(None, "filt", "slab", None, None),
    )
    out_specs = (
        P(None, "filt", "slab", None, None),
        P(None, "filt", None, None, None),
        P(None, "filt", None, None, None),
    )
    return jax.shard_map(
        on_device, mesh=mesh, in_specs=in_specs, out_specs=out_specs, check_vma=False
    )
```

profile of v0, /device:TPU:1, one launch (start us, length us, event | category | flops | bytes accessed | tf_op | source)
XLA Modules:
  0.0 759.8 jit_solution(5557039012614442161)
XLA Ops:
  7.2 0.9 fusion.16
  8.1 5.4 collective-permute-start
  13.5 8.3 %collective-permute-start.1 = (bf16[2,4,2,8,256]{4,3,2,1,0:T(8,128)(2,1)S(1)}, bf16[2,4,2,8,256]{4,3,2,1,0:T(8,128)(2,1)S(1)}, u32[]{:S(2)}, u32[]{:S(2)}) collective-permute-start(bf16[2,4,2,8,256]{4,3,2,1,0:T(8,128)(2,1)S(1)} %get-tuple-element.21), channel_id=1, source_target_pairs={{16,0},{32,16},{48,32},{64,48},{80,64},{96,80},{112,96},{128,112},... | collective-permute-start | bytes 196616 | tf_op jit(solution)/shard_map/ppermute | solution.py:15
  21.9 0.9 collective-permute-done.1
  22.7 0.9 pad_maximum_fusion
  23.7 0.7 copy.90
  24.5 110.2 %all-gather.3.cloned.1.call-done = bf16[2,64,8,8,256]{4,3,2,0,1:T(8,128)(2,1)} async-done(((bf16[2,4,8,8,256]{4,3,2,0,1:T(8,128)(2,1)}), bf16[2,64,8,8,256]{4,3,2,0,1:T(8,128)(2,1)}) %all-gather.3.cloned.1.call-update) | async-done | bytes 4194320 | tf_op jit(solution)/shard_map/all_gather | solution.py:57
  134.7 9.2 %copy.91 = bf16[2,64,8,8,256]{1,4,0,3,2:T(8,128)(2,1)} copy(bf16[2,64,8,8,256]{4,3,2,0,1:T(8,128)(2,1)} %all-gather.3.cloned.1.call-done) | data formatting | bytes 8388608 | tf_op jit(solution)/shard_map/all_gather | solution.py:57
  143.9 1.8 slice.30
  145.7 10.6 %fusion.1 = bf16[64,8,8,2,8,33]{0,5,4,3,2,1:T(8,128)(2,1)} fusion(bf16[64,8,8,2,7,1]{0,5,4,3,2,1:T(2,128)(2,1)S(1)} %slice.30, bf16[64,8,8,2,8,32]{0,5,4,3,2,1:T(8,128)(2,1)} %bitcast.60), kind=kLoop, calls=%fused_computation.2 | loop fusion | flops 12976128 | bytes 8634368 | tf_op jit(solution)/shard_map/conv_general_dilated | solution.py:34
  156.3 12.3 %multiply_convert_fusion = (bf16[4,4,16,16,8]{2,4,3,1,0:T(8,128)(2,1)S(1)}, f32[4,4,16,16,8]{2,4,3,1,0:T(8,128)S(1)}) fusion(bf16[64,8,2,2,2]{0,4,3,2,1:T(2,128)(2,1)S(1)} %copy-done.4, bf16[64,8,8,2,8,33]{0,5,4,3,2,1:T(8,128)(2,1)} %fusion.1), kind=kOutput, calls=%fused_computation.14 | convolution fusion | flops 33718272 | bytes 4530176 | tf_op jit(solution)/shard_map/conv_general_dilated | solution.py:34
  170.2 86.1 %all-gather.5.cloned.1.call-done = bf16[2,128,4,4,128]{4,3,2,0,1:T(4,128)(2,1)} async-done(((bf16[2,8,4,4,128]{4,3,2,0,1:T(4,128)(2,1)}), bf16[2,128,4,4,128]{4,3,2,0,1:T(4,128)(2,1)}) %all-gather.5.cloned.1.call-update) | async-done | bytes 1048592 | tf_op jit(solution)/shard_map/all_gather | solution.py:60
  256.3 2.8 copy.117
  259.1 0.8 pad.5.clone
  260.0 1.1 fusion.5
  261.2 16.2 %fusion.6 = f32[2,4,16,17,8]{2,4,3,1,0:T(8,128)S(1)} fusion(bf16[128,8,3,3,3]{0,1,4,3,2:T(8,128)(2,1)S(1)} %copy-done, bf16[128,4,4,2,8,19]{0,3,5,4,2,1:T(2,128)(2,1)S(1)} %fusion.5), kind=kOutput, calls=%fused_computation.9 | convolution fusion | flops 100270080 | bytes 1370112 | tf_op jit(solution)/shard_map/conv_general_dilated | solution.py:63
  278.6 7.7 %collective-permute-start.2 = (bf16[2,8,1,4,128]{4,0,1,3,2:T(2,128)(2,1)S(1)}, bf16[2,8,1,4,128]{4,0,1,3,2:T(2,128)(2,1)S(1)}, u32[]{:S(2)}, u32[]{:S(2)}) collective-permute-start(bf16[2,8,1,4,128]{4,0,1,3,2:T(2,128)(2,1)S(1)} %get-tuple-element.22), channel_id=1, source_target_pairs={{0,16},{16,32},{32,48},{48,64},{64,80},{80,96},{96,112},{112,128},... | collective-permute-start | bytes 49160 | tf_op jit(solution)/shard_map/ppermute | solution.py:14
  286.3 1.9 collective-permute-start.3
  288.2 1.3 dynamic-slice
  290.2 1.2 collective-permute-done.3
  292.7 0.9 copy.105
  293.6 2.1 convolution_select_fusion
  296.2 1.3 copy.107
  298.2 14.8 %copy.111 = bf16[2,64,8,8,256]{1,0,4,3,2:T(2,128)(2,1)} copy(bf16[2,64,8,8,256]{4,3,2,0,1:T(8,128)(2,1)} %all-gather.3.cloned.1.call-done) | data formatting | bytes 8388608 | tf_op jit(solution)/shard_map/all_gather | solution.py:57
  314.4 1.2 copy.113
  315.6 8.2 %fusion.19 = f32[128,8,3,3,3]{0,1,4,3,2:T(8,128)} fusion(bf16[2,128,4,4,128]{1,0,4,3,2:T(2,128)(2,1)S(1)} %copy.113, bf16[2,8,2,4,128]{1,0,4,3,2:T(2,128)(2,1)S(1)} %copy.114), kind=kOutput, calls=%fused_computation.35 | convolution fusion | flops 93880320 | bytes 1191936 | tf_op jit(solution)/shard_map/conv_general_dilated | solution.py:77
  323.8 128.9 %all-reduce.6.cloned.1.call-done = f32[2,128,2,4,128]{4,3,2,0,1:T(4,128)} async-done(((f32[2,128,2,4,128]{4,3,2,0,1:T(4,128)}), f32[2,128,2,4,128]{4,3,2,0,1:T(4,128)}) %all-reduce.6.cloned.1.call-update) | async-done | bytes 1048592
  452.7 0.8 constant_dynamic-slice_fusion
  453.9 7.1 fusion.18
  461.0 163.7 %psum.14 = f32[64,8,2,2,2]{0,1,4,3,2:T(8,128)S(1)} all-reduce(f32[64,8,2,2,2]{0,1,4,3,2:T(8,128)S(1)} %fusion.18), channel_id=1, replica_groups=mesh['slab'=48,'filt'=16] {'slab'}, use_global_device_ids=true, to_apply=%region_1.2 | all-reduce | flops 4096 | bytes 32768 | tf_op jit(solution)/shard_map/psum | solution.py:95
  625.4 126.4 %all-reduce.4.cloned.1.call-done = f32[128,8,3,3,3]{0,1,4,3,2:T(8,128)} async-done(((f32[128,8,3,3,3]{0,1,4,3,2:T(8,128)}), f32[128,8,3,3,3]{0,1,4,3,2:T(8,128)}) %all-reduce.4.cloned.1.call-update) | async-done | bytes 110608 | tf_op jit(solution)/shard_map/psum | solution.py:95
  751.8 1.5 copy.140
  (51 shorter events, 7.9 us)
Async XLA Ops:
  7.2 254.0 %copy-start = (bf16[128,8,3,3,3]{0,1,4,3,2:T(8,128)(2,1)S(1)}, bf16[128,8,3,3,3]{0,1,4,3,2:T(8,128)(2,1)}, u32[]{:S(2)}) copy-start(bf16[128,8,3,3,3]{0,1,4,3,2:T(8,128)(2,1)} %param.6) | copy-start | bytes 165892
  7.2 127.5 %all-gather.3.cloned.1.call-start = ((), (), s32[]{:S(2)}) async-start(), calls=%async_computation | async-start | bytes 4456448 | tf_op jit(solution)/shard_map/all_gather | solution.py:57
  8.1 13.7 %collective-permute-start = (bf16[2,4,2,8,256]{4,3,2,1,0:T(8,128)(2,1)S(1)}, bf16[2,4,2,8,256]{4,3,2,1,0:T(8,128)(2,1)S(1)}, u32[]{:S(2)}, u32[]{:S(2)}) collective-permute-start(bf16[2,4,2,8,256]{4,3,2,1,0:T(8,128)(2,1)S(1)} %get-tuple-element.20), channel_id=1, source_target_pairs={{0,16},{16,32},{32,48},{48,64},{64,80},{80,96},{96,112},{112,128},... | collective-permute-start | bytes 196616 | tf_op jit(solution)/shard_map/ppermute | solution.py:14
  13.5 9.2 %collective-permute-start.1 = (bf16[2,4,2,8,256]{4,3,2,1,0:T(8,128)(2,1)S(1)}, bf16[2,4,2,8,256]{4,3,2,1,0:T(8,128)(2,1)S(1)}, u32[]{:S(2)}, u32[]{:S(2)}) collective-permute-start(bf16[2,4,2,8,256]{4,3,2,1,0:T(8,128)(2,1)S(1)} %get-tuple-element.21), channel_id=1, source_target_pairs={{16,0},{32,16},{48,32},{64,48},{80,64},{96,80},{112,96},{128,112},... | collective-permute-start | bytes 196616 | tf_op jit(solution)/shard_map/ppermute | solution.py:15
  24.4 231.9 %all-gather.5.cloned.1.call-start = ((), (), s32[]{:S(2)}) async-start(), calls=%async_computation.1 | async-start | bytes 1114112 | tf_op jit(solution)/shard_map/all_gather | solution.py:60
  145.7 10.6 %copy-start.4 = (bf16[64,8,2,2,2]{0,4,3,2,1:T(2,128)(2,1)S(1)}, bf16[64,8,2,2,2]{0,4,3,2,1:T(2,128)(2,1)}, u32[]{:S(2)}) copy-start(bf16[64,8,2,2,2]{0,4,3,2,1:T(2,128)(2,1)} %param.5) | copy-start | bytes 24580
  170.0 282.7 %all-reduce.6.cloned.1.call-start = ((), (), s32[]{:S(2)}) async-start(), calls=%async_computation.3 | async-start | bytes 2097152
  261.2 16.7 %copy-start.3 = (pred[16,17]{1,0:T(8,128)(4,1)S(1)}, pred[16,17]{1,0:T(8,128)(4,1)}, u32[]{:S(2)}) copy-start(pred[16,17]{1,0:T(8,128)(4,1)} %constant.20) | copy-start | bytes 820
  277.4 1.1 copy-start.2
  278.6 11.6 %collective-permute-start.2 = (bf16[2,8,1,4,128]{4,0,1,3,2:T(2,128)(2,1)S(1)}, bf16[2,8,1,4,128]{4,0,1,3,2:T(2,128)(2,1)S(1)}, u32[]{:S(2)}, u32[]{:S(2)}) collective-permute-start(bf16[2,8,1,4,128]{4,0,1,3,2:T(2,128)(2,1)S(1)} %get-tuple-element.22), channel_id=1, source_target_pairs={{0,16},{16,32},{32,48},{48,64},{64,80},{80,96},{96,112},{112,128},... | collective-permute-start | bytes 49160 | tf_op jit(solution)/shard_map/ppermute | solution.py:14
  286.3 5.1 collective-permute-start.3
  292.1 1.5 copy-start.5
  297.5 454.2 %all-reduce.4.cloned.1.call-start = ((), (), s32[]{:S(2)}) async-start(), calls=%async_computation.2 | async-start | bytes 221184 | tf_op jit(solution)/shard_map/psum | solution.py:95
  298.2 16.2 %copy-start.1 = (bf16[2,128,4,4,128]{4,3,2,0,1:T(4,128)(2,1)S(1)}, bf16[2,128,4,4,128]{4,3,2,0,1:T(4,128)(2,1)}, u32[]{:S(2)}) copy-start(bf16[2,128,4,4,128]{4,3,2,0,1:T(4,128)(2,1)} %all-gather.5.cloned.1.call-done) | copy-start | bytes 3145732
Sparse Core Ops, SparseCore 0:
  24.5 110.0 all-gather.2
  170.1 86.1 all-gather.4
  297.6 154.9 all-reduce.5
  456.6 295.0 all-reduce.3
where the time goes:
time: 763 us; the launch traced here: 760 us
  waiting for transfers between devices  454 us (60%)
  blocking collectives  164 us (21%)
  matrix products  45.8 us (6%)
  local copies, waits for them, and re-layouts  44.6 us (6%)
  starting transfers between devices  23.7 us (3%)
  between operations  14.8 us (2%)
  other arithmetic  13.7 us (2%)
    psum x1, blocking collectives, on_device(): weight_one, weight_two = lax.psum((weight_one, weight_two), 'slab')  164 us
    unnamed x5, waiting for transfers between devices  129 us
    psum x1, waiting for transfers between devices, on_device(): weight_one, weight_two = lax.psum((weight_one, weight_two), 'slab')  126 us
    all_gather x1, waiting for transfers between devices, on_device(): all_inputs = lax.all_gather(extended, 'filt', axis=1, tiled=True)  110 us
    all_gather x1, waiting for transfers between devices, on_device(): hidden_ext = lax.all_gather(own_hidden, 'filt', axis=1, tiled=True)  86.1 us
    all_gather x2, local copies, waits for them, and re-layouts, on_device(): all_inputs = lax.all_gather(extended, 'filt', axis=1, tiled=True)  24 us
    conv_general_dilated x1, matrix products, on_device(): lax.conv_general_dilated(hidden_pad, second_weight, (1, 1, 1), 'VALID', d...  16.2 us
  transfers between devices with their start and end apart: 8, of which 6 were waited for; matrix products, arithmetic and copies ran while one was open for 5% of the time, Pallas kernels for 0%

commit v1 on v0

v1 whole, which is shorter than its diff:
```python
import functools

import jax
import jax.numpy as jnp
from jax import lax
from jax.experimental import pallas as pl
from jax.experimental.pallas import tpu as pltpu
from jax.sharding import PartitionSpec as P

BF = jnp.bfloat16
F32 = jnp.float32
MESH = pl.DeviceIdType.MESH
VMEM = pl.BlockSpec(memory_space=pltpu.VMEM)


def silu_value(values):
    return values * jax.nn.sigmoid(values)


def silu_slope(values):
    logistic = jax.nn.sigmoid(values)
    return logistic * (1.0 + values * (1.0 - logistic))


def exchange_kernel(axis, n, kinds, *refs):
    count = len(kinds)
    ins, outs = refs[:count], refs[count : 2 * count]
    send_sem, recv_sem, own_sem = refs[2 * count :]
    me = lax.axis_index(axis)
    barrier = pltpu.get_barrier_semaphore()

    def greet(r, carry):
        pl.semaphore_signal(
            barrier, inc=1, device_id={axis: lax.rem(me + r, n)}, device_id_type=MESH
        )
        return carry

    lax.fori_loop(1, n, greet, 0)
    pl.semaphore_wait(barrier, n - 1)

    def copy(i, r):
        to = lax.rem(me + r, n)
        source = ins[i].at[to] if kinds[i] else ins[i]
        return pltpu.make_async_remote_copy(
            src_ref=source,
            dst_ref=outs[i].at[me],
            send_sem=send_sem.at[i, r],
            recv_sem=recv_sem.at[i, r],
            device_id={axis: to},
            device_id_type=MESH,
        )

    def start(r, carry):
        for i in range(count):
            copy(i, r).start()
        return carry

    lax.fori_loop(1, n, start, 0)
    own = [
        pltpu.make_async_copy(
            ins[i].at[me] if kinds[i] else ins[i], outs[i].at[me], own_sem.at[i]
        )
        for i in range(count)
    ]
    for one in own:
        one.start()
    for one in own:
        one.wait()

    def finish(r, carry):
        for i in range(count):
            copy(i, r).wait()
        return carry

    lax.fori_loop(1, n, finish, 0)


def exchange(axis, arrays, kinds, number, name):
    n = lax.axis_size(axis)
    count = len(arrays)
    shapes = [
        jax.ShapeDtypeStruct(a.shape if kind else (n,) + a.shape, a.dtype)
        for a, kind in zip(arrays, kinds)
    ]
    return pl.pallas_call(
        functools.partial(exchange_kernel, axis, n, kinds),
        out_shape=shapes,
        in_specs=[VMEM] * count,
        out_specs=[VMEM] * count,
        scratch_shapes=[
            pltpu.SemaphoreType.DMA((count, n)),
            pltpu.SemaphoreType.DMA((count, n)),
            pltpu.SemaphoreType.DMA((count,)),
        ],
        compiler_params=pltpu.CompilerParams(
            collective_id=number, has_side_effects=True
        ),
        name=name,
    )(*arrays)


def halo_kernel(axis, n, up_ref, down_ref, below_ref, above_ref, send_sem, recv_sem):
    me = lax.axis_index(axis)
    after, before = lax.rem(me + 1, n), lax.rem(me + n - 1, n)
    barrier = pltpu.get_barrier_semaphore()
    for peer in (before, after):
        pl.semaphore_signal(
            barrier, inc=1, device_id={axis: peer}, device_id_type=MESH
        )
    pl.semaphore_wait(barrier, 2)
    copies = [
        pltpu.make_async_remote_copy(
            src_ref=source,
            dst_ref=target,
            send_sem=send_sem.at[i],
            recv_sem=recv_sem.at[i],
            device_id={axis: peer},
            device_id_type=MESH,
        )
        for i, (source, target, peer) in enumerate(
            ((up_ref, below_ref, after), (down_ref, above_ref, before))
        )
    ]
    for one in copies:
        one.start()
    for one in copies:
        one.wait()


def halo(axis, up, down, number, name):
    n = lax.axis_size(axis)
    return pl.pallas_call(
        functools.partial(halo_kernel, axis, n),
        out_shape=[jax.ShapeDtypeStruct(a.shape, a.dtype) for a in (up, down)],
        in_specs=[VMEM] * 2,
        out_specs=[VMEM] * 2,
        scratch_shapes=[
            pltpu.SemaphoreType.DMA((2,)),
            pltpu.SemaphoreType.DMA((2,)),
        ],
        compiler_params=pltpu.CompilerParams(
            collective_id=number, has_side_effects=True
        ),
        name=name,
    )(up, down)


def compute(kernel, shapes, arrays, name, scratch=(), scalar=None):
    specs = [VMEM] * len(arrays)
    if scalar is not None:
        arrays = [scalar] + list(arrays)
        specs = [pl.BlockSpec(memory_space=pltpu.SMEM)] + specs
    return pl.pallas_call(
        kernel,
        out_shape=[jax.ShapeDtypeStruct(s, d) for s, d in shapes],
        in_specs=specs,
        out_specs=[VMEM] * len(shapes),
        scratch_shapes=list(scratch),
        name=name,
    )(*arrays)


def one_hot(source_of_row, size):
    row = lax.broadcasted_iota(jnp.int32, (size, size), 0)
    column = lax.broadcasted_iota(jnp.int32, (size, size), 1)
    return jnp.where(source_of_row(row) == column, 1.0, 0.0).astype(BF)


def pieces_kernel(x_ref, out_ref):
    def source(o):
        b, d, h = o >> 7, (o >> 6) & 1, (o >> 4) & 3
        c, i, j = (o >> 2) & 3, (o >> 1) & 1, o & 1
        return (b << 7) + (c << 5) + ((2 * d + i) << 3) + 2 * h + j

    rows = one_hot(source, 256)
    row = lax.broadcasted_iota(jnp.int32, (256, 256), 0)
    column = lax.broadcasted_iota(jnp.int32, (256, 256), 1)
    columns = jnp.where(row == 2 * (column & 127) + (column >> 7), 1.0, 0.0).astype(BF)
    half = jnp.dot(rows, x_ref[...], preferred_element_type=F32).astype(BF)
    out_ref[...] = jnp.dot(half, columns, preferred_element_type=F32).astype(BF)


def first_kernel(x_ref, w_ref, pre_ref, hidden_ref):
    pre = jnp.dot(w_ref[:, :256], x_ref[:, :128], preferred_element_type=F32)
    pre += jnp.dot(w_ref[:, 256:], x_ref[:, 128:], preferred_element_type=F32)
    pre_ref[...] = pre
    hidden_ref[...] = silu_value(pre).astype(BF)


def shifted(values, by):
    if by == 0:
        return values
    lane = lax.broadcasted_iota(jnp.int32, values.shape, 1)
    rolled = pltpu.roll(values, (-by) % 128, 1)
    return jnp.where(lane == (127 if by > 0 else 0), 0.0, rolled)


def tap(a, e, g):
    return ((a * 3 + e) * 3 + g) * 8


def second_kernel(hidden_ref, w_ref, own_ref, up_ref, down_ref, y_ref):
    for q in range(16):
        y_ref[q] = jnp.dot(w_ref[...], hidden_ref[q], preferred_element_type=F32)
    for b in range(2):
        for d in range(-1, 3):
            for h in range(4):
                total = None
                for g in range(3):
                    part = None
                    for a in range(3):
                        plane = d + a - 1
                        if plane < 0 or plane > 1:
                            continue
                        for e in range(3):
                            row = h + e - 1
                            if row < 0 or row > 3:
                                continue
                            at = tap(a, e, g)
                            term = y_ref[b * 8 + plane * 4 + row, at : at + 8, :]
                            part = term if part is None else part + term
                    part = shifted(part, g - 1)
                    total = part if total is None else total + part
                if d < 0:
                    down_ref[b * 4 + h] = total
                elif d > 1:
                    up_ref[b * 4 + h] = total
                else:
                    own_ref[b * 8 + d * 4 + h] = total


def result_kernel(
    edge_ref, own_ref, below_ref, above_ref, grad_ref, result_ref, sg_ref, up_ref, down_ref
):
    low, high = edge_ref[0] > 0, edge_ref[1] > 0
    for b in range(2):
        for d in range(2):
            for h in range(4):
                q, r = b * 8 + d * 4 + h, b * 4 + h
                other = below_ref[r] if d == 0 else above_ref[r]
                pre = own_ref[q] + jnp.where(low if d == 0 else high, other, 0.0)
                result_ref[q] = silu_value(pre).astype(BF)
                grad = (grad_ref[q].astype(F32) * silu_slope(pre)).astype(BF)
                sg_ref[q] = grad
                if d == 0:
                    down_ref[r] = grad
                else:
                    up_ref[r] = grad


def back_kernel(
    edge_ref, sg_ref, below_ref, above_ref, w_ref, hidden_ref, mid_ref, w2_ref, s_ref
):
    low, high = edge_ref[0] > 0, edge_ref[1] > 0
    total = None
    for b in range(2):
        views = {}
        for plane in range(-1, 3):
            for h in range(4):
                if plane < 0:
                    value = jnp.where(low, below_ref[b * 4 + h].astype(F32), 0.0)
                elif plane > 1:
                    value = jnp.where(high, above_ref[b * 4 + h].astype(F32), 0.0)
                else:
                    value = sg_ref[b * 8 + plane * 4 + h].astype(F32)
                for g in range(3):
                    views[plane, h, g] = shifted(value, 1 - g)
        for d in range(2):
            for h in range(4):
                q = b * 8 + d * 4 + h
                for a in range(3):
                    for e in range(3):
                        row = h - e + 1
                        for g in range(3):
                            at = tap(a, e, g)
                            if row < 0 or row > 3:
                                block = jnp.zeros((8, 128), F32)
                            else:
                                block = views[d - a + 1, row, g]
                            s_ref[q, at : at + 8, :] = block
    for q in range(16):
        taps = s_ref[q].astype(BF)
        mid_ref[q] = jnp.dot(w_ref[...], taps, preferred_element_type=F32).astype(BF)
        part = lax.dot_general(
            taps, hidden_ref[q], (((1,), (1,)), ((), ())), preferred_element_type=F32
        )
        total = part if total is None else total + part
    w2_ref[...] = total


def first_back_kernel(parts_ref, pre_ref, x_ref, w1_ref):
    mid = parts_ref[0].astype(F32)
    for p in range(1, 16):
        mid += parts_ref[p].astype(F32)
    grad = (mid * silu_slope(pre_ref[...])).astype(BF)
    for k in range(2):
        w1_ref[:, k * 256 : (k + 1) * 256] = lax.dot_general(
            grad,
            x_ref[:, k * 128 : (k + 1) * 128],
            (((1,), (1,)), ((), ())),
            preferred_element_type=F32,
        )


def sum_kernel(parts_ref, out_ref):
    total = parts_ref[0]
    for p in range(1, parts_ref.shape[0]):
        total += parts_ref[p]
    out_ref[...] = total


def sum_blocks(parts, name):
    return compute(sum_kernel, [(parts.shape[1:], parts.dtype)], [parts], name)[0]


def on_device(volume, first_weight, second_weight, out_grad):
    slabs = lax.axis_size("slab")
    me = lax.axis_index("slab")
    edge = jnp.stack([me > 0, me < slabs - 1]).astype(jnp.int32)
    w_one = first_weight.transpose(1, 4, 0, 2, 3).reshape(8, 512)
    w_two = second_weight.transpose(2, 3, 4, 1, 0).reshape(216, 128)
    w_two_t = second_weight.transpose(0, 2, 3, 4, 1).reshape(128, 216)
    grad_rows = out_grad.transpose(0, 2, 3, 1, 4).reshape(16, 8, 128)

    (pieces,) = compute(
        pieces_kernel, [((256, 256), BF)], [volume.reshape(256, 256)], "pieces"
    )
    x_all, w_all = exchange(
        "filt", [pieces.reshape(16, 16, 256), w_one], (1, 0), 1, "send_volume"
    )
    x_all, w_all = x_all.reshape(256, 256), w_all.reshape(128, 512)
    pre, hidden_own = compute(
        first_kernel, [((128, 128), F32), ((128, 128), BF)], [x_all, w_all], "first"
    )
    (hidden,) = exchange("filt", [hidden_own], (0,), 2, "send_hidden")
    own, up, down = compute(
        second_kernel,
        [((16, 8, 128), F32), ((8, 8, 128), F32), ((8, 8, 128), F32)],
        [hidden, w_two],
        "second",
        scratch=[pltpu.VMEM((16, 216, 128), F32)],
    )
    below, above = halo("slab", up, down, 3, "send_rims")
    result, sg, up, down = compute(
        result_kernel,
        [((16, 8, 128), BF), ((16, 8, 128), BF), ((8, 8, 128), BF), ((8, 8, 128), BF)],
        [own, below, above, grad_rows],
        "result",
        scalar=edge,
    )
    below, above = halo("slab", up, down, 4, "send_grad_rims")
    mid, w2_part = compute(
        back_kernel,
        [((16, 128, 128), BF), ((216, 128), F32)],
        [sg, below, above, w_two_t, hidden],
        "back",
        scratch=[pltpu.VMEM((16, 216, 128), F32)],
        scalar=edge,
    )
    (mid_parts,) = exchange("filt", [mid], (1,), 5, "send_mid")
    (w1_part,) = compute(
        first_back_kernel, [((128, 512), F32)], [mid_parts, pre, x_all], "first_back"
    )
    (w1_parts,) = exchange("filt", [w1_part.reshape(16, 8, 512)], (1,), 6, "send_w1")
    w1_own = sum_blocks(w1_parts, "sum_w1")

    rows = jnp.concatenate([w2_part, w1_own.reshape(32, 128)], axis=0)
    blocks = -(-rows.shape[0] // (8 * slabs)) * slabs
    rows = jnp.pad(rows, ((0, blocks * 8 - rows.shape[0]), (0, 0)))
    per = blocks * 8 // slabs
    (parts,) = exchange("slab", [rows.reshape(slabs, per, 128)], (1,), 7, "scatter")
    summed = sum_blocks(parts, "sum_slabs")
    (rows,) = exchange("slab", [summed], (0,), 8, "gather")
    rows = rows.reshape(blocks * 8, 128)
    weight_two = rows[:216].reshape(3, 3, 3, 8, 128).transpose(4, 3, 0, 1, 2)
    weight_one = rows[216:248].reshape(8, 2, 64, 2, 2).transpose(2, 0, 3, 4, 1)
    result = result.reshape(2, 2, 4, 8, 128).transpose(0, 3, 1, 2, 4)
    return (result, weight_one, weight_two)


def solution(mesh):
    in_specs = (
        P(None, "filt", "slab", None, None),
        P(None, "filt", None, None, None),
        P(None, "filt", None, None, None),
        P(None, "filt", "slab", None, None),
    )
    out_specs = (
        P(None, "filt", "slab", None, None),
        P(None, "filt", None, None, None),
        P(None, "filt", None, None, None),
    )
    return jax.shard_map(
        on_device, mesh=mesh, in_specs=in_specs, out_specs=out_specs, check_vma=False
    )
```

time: 763 us -> 166 us (0.22)
  waiting for transfers between devices: 454 us -> 0 us
  blocking collectives: 164 us -> 0 us
  Pallas kernels: 0 us -> 153 us
  matrix products: 45.8 us -> 0 us
  local copies, waits for them, and re-layouts: 44.6 us -> 9.28 us
  starting transfers between devices: 23.7 us -> 0 us
  between operations: 14.8 us -> 0.75 us
  other arithmetic: 13.7 us -> 1.31 us
    all_gather x2 -> x0, waiting for transfers between devices: 196 us -> none  [the longest x1 110 us: on_device(): all_inputs = lax.all_gather(extended, 'filt', axis=1, tiled=True)]
    psum x1 -> x0, blocking collectives: 164 us -> none  [on_device(): weight_one, weight_two = lax.psum((weight_one, weight_two), 'slab')]
    pallas_call x0 -> x16, Pallas kernels: none -> 153 us  [the longest x6 113 us: exchange(): pl.pallas_call(functools.partial(exchange_kernel, axis, n, kinds), out_sh...]
    unnamed x5 -> x0, waiting for transfers between devices: 129 us -> none
    psum x1 -> x0, waiting for transfers between devices: 126 us -> none  [on_device(): weight_one, weight_two = lax.psum((weight_one, weight_two), 'slab')]
    conv_general_dilated x5 -> x0, matrix products: 45.8 us -> none  [the longest x1 16.2 us: on_device(): lax.conv_general_dilated(hidden_pad, second_weight, (1, 1, 1), 'VALID', d...]
    all_gather x4 -> x0, local copies, waits for them, and re-layouts: 26.1 us -> none  [the longest x2 24 us: on_device(): all_inputs = lax.all_gather(extended, 'filt', axis=1, tiled=True)]
    ppermute x4 -> x0, starting transfers between devices: 23.3 us -> none  [the longest x2 13.1 us: padded(): before = lax.ppermute(last, axis, up)]
  transfers between devices with their start and end apart: 8 -> 0, of which waited for: 6 -> 0; matrix products, arithmetic and copies ran while one was open for 5% -> 0% of each run, Pallas kernels for 0% -> 0%
where the time goes in v1:
time: 166 us; the launch traced here: 164 us
  Pallas kernels  153 us (92%)
  local copies, waits for them, and re-layouts  9.28 us (6%)
    pallas_call x6, Pallas kernels, exchange(): pl.pallas_call(functools.partial(exchange_kernel, axis, n, kinds), out_sh...  113 us
    pallas_call x2, Pallas kernels, halo(): pl.pallas_call(functools.partial(halo_kernel, axis, n), out_shape=[jax.Sh...  24.9 us
    pallas_call x8, Pallas kernels, compute(): pl.pallas_call(kernel, out_shape=[jax.ShapeDtypeStruct(s, d) for s, d in...  15.3 us

profile of v1, /device:TPU:1, one launch (start us, length us, event | category | flops | bytes accessed | tf_op | source)
XLA Modules:
  0.0 164.2 jit_solution(12560278534894846124)
XLA Ops:
  0.6 0.0 copy-start
  0.7 0.6 add_convert_fusion.edge_ref
  1.3 1.4 copy.14
  2.6 0.0 copy-done
  2.6 0.7 copy.16.w_ref
  3.4 1.9 %pieces.1 = bf16[256,256]{1,0:T(8,128)(2,1)} custom-call(bf16[256,256]{1,0:T(8,128)(2,1)} %bitcast.36), custom_call_target="tpu_custom_call" | custom-call | tf_op jit(solution)/shard_map/pieces/pallas_call | solution.py:153
  5.3 0.0 copy-done.2
  5.3 0.1 copy.12
  5.4 0.7 copy.13.refs_1_
  6.1 15.9 %send_volume.1 = (bf16[16,16,256]{2,1,0:T(8,128)(2,1)}, bf16[16,8,512]{2,1,0:T(8,128)(2,1)}) custom-call(bf16[16,16,256]{2,1,0:T(8,128)(2,1)} %bitcast.31, bf16[8,512]{1,0:T(8,128)(2,1)} %copy.13.refs_1_), custom_call_target="tpu_custom_call" | custom-call | tf_op jit(solution)/shard_map/send_volume/pallas_call | solution.py:85
  22.0 1.8 %first.1 = (f32[128,128]{1,0:T(8,128)}, bf16[128,128]{1,0:T(8,128)(2,1)}) custom-call(bf16[256,256]{1,0:T(8,128)(2,1)} %bitcast.29, bf16[128,512]{1,0:T(8,128)(2,1)} %bitcast.37), custom_call_target="tpu_custom_call" | custom-call | tf_op jit(solution)/shard_map/first/pallas_call | solution.py:153
  23.8 20.2 %send_hidden.1.hidden_ref = bf16[16,128,128]{2,1,0:T(8,128)(2,1)} custom-call(bf16[128,128]{1,0:T(8,128)(2,1)} %get-tuple-element.22.refs_0_), custom_call_target="tpu_custom_call" | custom-call | tf_op jit(solution)/shard_map/send_hidden/pallas_call | solution.py:85
  43.9 2.1 %second.1 = (f32[16,8,128]{2,1,0:T(8,128)}, f32[8,8,128]{2,1,0:T(8,128)}, f32[8,8,128]{2,1,0:T(8,128)}) custom-call(bf16[16,128,128]{2,1,0:T(8,128)(2,1)} %send_hidden.1.hidden_ref, bf16[216,128]{1,0:T(8,128)(2,1)} %bitcast.33), custom_call_target="tpu_custom_call" | custom-call | tf_op jit(solution)/shard_map/second/pallas_call | solution.py:153
  46.1 17.4 %send_rims.1 = (f32[8,8,128]{2,1,0:T(8,128)}, f32[8,8,128]{2,1,0:T(8,128)}) custom-call(f32[8,8,128]{2,1,0:T(8,128)} %get-tuple-element.24.up_ref, f32[8,8,128]{2,1,0:T(8,128)} %get-tuple-element.25.down_ref), custom_call_target="tpu_custom_call" | custom-call | tf_op jit(solution)/shard_map/send_rims/pallas_call | solution.py:132
  63.5 1.5 result.1
  65.1 1.4 copy.19
  66.4 7.5 %send_grad_rims.1 = (bf16[8,8,128]{2,1,0:T(8,128)(2,1)}, bf16[8,8,128]{2,1,0:T(8,128)(2,1)}) custom-call(bf16[8,8,128]{2,1,0:T(8,128)(2,1)} %get-tuple-element.30.up_ref, bf16[8,8,128]{2,1,0:T(8,128)(2,1)} %get-tuple-element.31.down_ref), custom_call_target="tpu_custom_call" | custom-call | tf_op jit(solution)/shard_map/send_grad_rims/pallas_call | solution.py:132
  74.0 2.8 %back.1 = (bf16[16,128,128]{2,1,0:T(8,128)(2,1)}, f32[216,128]{1,0:T(8,128)}) custom-call(s32[2]{0:T(128)} %add_convert_fusion.edge_ref, bf16[16,8,128]{2,1,0:T(8,128)(2,1)} %get-tuple-element.29.sg_ref, bf16[8,8,128]{2,1,0:T(8,128)(2,1)} %get-tuple-element.32.below_ref, bf16[8,8,128]{2,1,0:T(8,128)(2,1)} %get-tuple-element.33.above_ref, ...), custom_call_target="tpu_custom_call" | custom-call | tf_op jit(solution)/shard_map/back/pallas_call | solution.py:153
  76.7 20.3 %send_mid.1.parts_ref = bf16[16,128,128]{2,1,0:T(8,128)(2,1)} custom-call(bf16[16,128,128]{2,1,0:T(8,128)(2,1)} %get-tuple-element.35.refs_0_), custom_call_target="tpu_custom_call" | custom-call | tf_op jit(solution)/shard_map/send_mid/pallas_call | solution.py:85
  97.0 2.0 %first_back.1 = f32[128,512]{1,0:T(8,128)} custom-call(bf16[16,128,128]{2,1,0:T(8,128)(2,1)} %send_mid.1.parts_ref, f32[128,128]{1,0:T(8,128)} %get-tuple-element.36.pre_ref, bf16[256,256]{1,0:T(8,128)(2,1)} %bitcast.30), custom_call_target="tpu_custom_call" | custom-call | tf_op jit(solution)/shard_map/first_back/pallas_call | solution.py:153
  99.1 14.3 %send_w1.1.parts_ref = f32[16,8,512]{2,1,0:T(8,128)} custom-call(f32[16,8,512]{2,1,0:T(8,128)} %bitcast.28), custom_call_target="tpu_custom_call" | custom-call | tf_op jit(solution)/shard_map/send_w1/pallas_call | solution.py:85
  113.4 0.0 copy-start.1
  113.4 1.6 sum_w1.1
  115.0 0.7 reshape.63
  115.8 0.7 fusion.refs_0_
  116.5 23.2 %scatter.1.parts_ref = f32[48,8,128]{2,1,0:T(8,128)} custom-call(f32[48,8,128]{2,1,0:T(8,128)} %fusion.refs_0_), custom_call_target="tpu_custom_call" | custom-call | tf_op jit(solution)/shard_map/scatter/pallas_call | solution.py:85
  139.6 1.6 sum_slabs.1.refs_0_
  141.2 18.7 %gather.1 = f32[48,8,128]{2,1,0:T(8,128)} custom-call(f32[8,128]{1,0:T(8,128)} %sum_slabs.1.refs_0_), custom_call_target="tpu_custom_call" | custom-call | tf_op jit(solution)/shard_map/gather/pallas_call | solution.py:85
  159.9 0.0 slice-start
  160.0 1.6 slice.9
  161.5 1.6 reshape.65
  163.1 1.1 copy.17
  (3 shorter events, 0.0 us)
Async XLA Ops:
  0.6 2.0 %copy-start = (bf16[128,8,3,3,3]{0,1,4,3,2:T(8,128)(2,1)S(1)}, bf16[128,8,3,3,3]{0,1,4,3,2:T(8,128)(2,1)}, u32[]{:S(2)}) copy-start(bf16[128,8,3,3,3]{0,1,4,3,2:T(8,128)(2,1)} %param.6) | copy-start | bytes 165892
  3.4 1.9 %copy-start.2 = (bf16[64,8,2,2,2]{0,4,3,2,1:T(2,128)(2,1)S(1)}, bf16[64,8,2,2,2]{0,4,3,2,1:T(2,128)(2,1)}, u32[]{:S(2)}) copy-start(bf16[64,8,2,2,2]{0,4,3,2,1:T(2,128)(2,1)} %param.5) | copy-start | bytes 24580
  113.4 2.3 %copy-start.1 = (f32[216,128]{1,0:T(8,128)S(1)}, f32[216,128]{1,0:T(8,128)}, u32[]{:S(2)}) copy-start(f32[216,128]{1,0:T(8,128)} %get-tuple-element.34) | copy-start | bytes 331780
  159.9 1.6 slice-start

commit v2 on v0

v2 whole, which is shorter than its diff:
```python
import functools

import jax
import jax.numpy as jnp
from jax import lax
from jax.experimental import pallas as pl
from jax.experimental.pallas import tpu as pltpu
from jax.sharding import PartitionSpec as P

BF = jnp.bfloat16
F32 = jnp.float32
MESH = pl.DeviceIdType.MESH
VMEM = pl.BlockSpec(memory_space=pltpu.VMEM)
TAPS = 27
W1_BLOCKS = 4


def silu_value(values):
    return values * jax.nn.sigmoid(values)


def silu_slope(values):
    logistic = jax.nn.sigmoid(values)
    return logistic * (1.0 + values * (1.0 - logistic))


def one_hot(source_of_row, size):
    row = lax.broadcasted_iota(jnp.int32, (size, size), 0)
    column = lax.broadcasted_iota(jnp.int32, (size, size), 1)
    return jnp.where(source_of_row(row) == column, 1.0, 0.0).astype(BF)


def piece_matrices():
    def source(o):
        b, d, h = o >> 7, (o >> 6) & 1, (o >> 4) & 3
        c, i, j = (o >> 2) & 3, (o >> 1) & 1, o & 1
        return (b << 7) + (c << 5) + ((2 * d + i) << 3) + 2 * h + j

    row = lax.broadcasted_iota(jnp.int32, (256, 256), 0)
    column = lax.broadcasted_iota(jnp.int32, (256, 256), 1)
    columns = jnp.where(row == 2 * (column & 127) + (column >> 7), 1.0, 0.0).astype(BF)
    return one_hot(source, 256), columns


def shifted(values, by):
    if by == 0:
        return values
    flat = values.reshape(-1, 128)
    lane = lax.broadcasted_iota(jnp.int32, flat.shape, 1)
    rolled = pltpu.roll(flat, (-by) % 128, 1)
    return jnp.where(lane == (127 if by > 0 else 0), 0.0, rolled).reshape(values.shape)


def tap(a, e, g):
    return ((a * 3 + e) * 3 + g) * 8


def nt_dot(a, b):
    return lax.dot_general(a, b, (((1,), (1,)), ((), ())), preferred_element_type=F32)


def remote(source, target, send, recv, axis, to):
    return pltpu.make_async_remote_copy(
        src_ref=source,
        dst_ref=target,
        send_sem=send,
        recv_sem=recv,
        device_id={axis: to},
        device_id_type=MESH,
    )


def repeat(low, high, step):
    lax.fori_loop(low, high, lambda i, carry: (step(i), carry)[1], 0)


class Scatter:
    def __init__(self, n, me, first, count, blocks, landing, total, out, sems):
        self.n, self.me, self.first = n, me, first
        self.owners, self.per = count
        self.blocks, self.landing, self.total, self.out = blocks, landing, total, out
        self.send_a, self.recv_a, self.send_b, self.recv_b = sems

    def owner(self, j):
        return lax.rem(self.first + j, self.n)

    def index(self):
        return lax.rem(self.me - self.first + self.n, self.n)

    def out_copy(self, j):
        return remote(
            self.blocks.at[pl.ds(j * self.per, self.per)],
            self.landing.at[self.me],
            self.send_a.at[j],
            self.recv_a.at[self.me],
            "slab",
            self.owner(j),
        )

    def in_copy(self, source):
        return remote(
            self.total,
            self.landing.at[source],
            self.send_a.at[0],
            self.recv_a.at[source],
            "slab",
            source,
        )

    def back_copy(self, r):
        at = self.index() * self.per
        return remote(
            self.total,
            self.out.at[pl.ds(at, self.per)],
            self.send_b.at[r],
            self.recv_b.at[self.index()],
            "slab",
            lax.rem(self.me + r, self.n),
        )

    def each_owner(self, step):
        def one(j):
            @pl.when(self.owner(j) != self.me)
            def _():
                step(j)

        repeat(0, self.owners, one)

    def start(self):
        self.each_owner(lambda j: self.out_copy(j).start())

    def reduce(self):
        @pl.when(self.index() < self.owners)
        def _():
            at = pl.ds(self.index() * self.per, self.per)

            def add(r, total):
                source = lax.rem(self.me + self.n - r, self.n)
                self.in_copy(source).wait_recv()
                return total + self.landing[source]

            total = lax.fori_loop(1, self.n, add, self.blocks[at])
            self.total[...] = total
            self.out[at] = total
            repeat(1, self.n, lambda r: self.back_copy(r).start())

    def finish(self):
        def arrive(j):
            remote(
                self.total,
                self.out.at[pl.ds(j * self.per, self.per)],
                self.send_b.at[0],
                self.recv_b.at[j],
                "slab",
                self.owner(j),
            ).wait_recv()

        self.each_owner(arrive)
        self.each_owner(lambda j: self.out_copy(j).wait_send())

        @pl.when(self.index() < self.owners)
        def _():
            repeat(1, self.n, lambda r: self.back_copy(r).wait_send())


def level_kernel(
    filts, slabs, two_count, one_count,
    x_ref, w1_ref, w2_ref, og_ref,
    result_ref, two_out, one_out,
    piece, x_all, w_all, hid, y, own, up, down, below, above,
    sg, sg_below, sg_above, view, s, mid, mid_in, dw1, dw1_in, w2_t, pre_ref,
    two, two_in, two_sum, one, one_in, one_sum,
    fs, fr, hs, hr, ts_a, tr_a, ts_b, tr_b, os_a, or_a, os_b, or_b,
):
    f, z = lax.axis_index("filt"), lax.axis_index("slab")
    barrier = pltpu.get_barrier_semaphore()

    def greet(axis, me, n):
        def one_peer(r):
            pl.semaphore_signal(
                barrier,
                inc=1,
                device_id={axis: lax.rem(me + r, n)},
                device_id_type=MESH,
            )

        repeat(1, n, one_peer)

    greet("filt", f, filts)
    greet("slab", z, slabs)

    def peer(r):
        return lax.rem(f + r, filts)

    def source(r):
        return lax.rem(f + filts - r, filts)

    def filt(i, r, block, target):
        return remote(block, target, fs.at[i, r], fr.at[i, r], "filt", peer(r))

    def to_all(step):
        repeat(1, filts, step)

    rows, columns = piece_matrices()
    half = jnp.dot(rows, x_ref[...], preferred_element_type=F32).astype(BF)
    cut = jnp.dot(half, columns, preferred_element_type=F32).astype(BF)
    piece[...] = cut.reshape(piece.shape)
    x_all[f] = piece[f]
    w_all[f] = w1_ref[...]
    pl.semaphore_wait(barrier, filts + slabs - 2)

    def send_x(r):
        filt(0, r, piece.at[peer(r)], x_all.at[f]).start()
        filt(1, r, w1_ref, w_all.at[f]).start()

    to_all(send_x)
    eye = one_hot(lambda o: o, 128)
    w2_t[...] = nt_dot(eye, w2_ref[...]).astype(BF)
    y[:, :, 0] = jnp.zeros((2, 2, 216, 128), F32)
    y[:, :, 5] = jnp.zeros((2, 2, 216, 128), F32)
    view[:, :, :, 0] = jnp.zeros((3, 2, 4, 8, 128), F32)
    view[:, :, :, 5] = jnp.zeros((3, 2, 4, 8, 128), F32)

    def get_x(r):
        filt(0, r, piece.at[peer(r)], x_all.at[source(r)]).wait_recv()
        filt(1, r, w1_ref, w_all.at[source(r)]).wait_recv()

    to_all(get_x)
    x = x_all[...].reshape(256, 256)
    w = w_all[...].reshape(128, 512)
    pre = jnp.dot(w[:, :256], x[:, :128], preferred_element_type=F32)
    pre += jnp.dot(w[:, 256:], x[:, 128:], preferred_element_type=F32)
    pre_ref[...] = pre
    hid[f] = silu_value(pre).astype(BF)
    to_all(lambda r: filt(2, r, hid.at[f], hid.at[f]).start())

    def spread(q):
        b, d, h = lax.div(q, 8), lax.rem(lax.div(q, 4), 2), lax.rem(q, 4)
        y[b, d, h + 1] = jnp.dot(w2_ref[...], hid[q], preferred_element_type=F32)

    spread(f)

    def get_hidden(r):
        filt(2, r, hid.at[f], hid.at[source(r)]).wait_recv()
        spread(source(r))

    to_all(get_hidden)
    for d in (-1, 2, 0, 1):
        total = None
        for g in range(3):
            part = None
            for a in range(3):
                plane = d + a - 1
                if plane < 0 or plane > 1:
                    continue
                for e in range(3):
                    at = tap(a, e, g)
                    term = y[:, plane, e : e + 4, at : at + 8, :]
                    part = term if part is None else part + term
            part = shifted(part, g - 1)
            total = part if total is None else total + part
        if d < 0:
            down[...] = total
        elif d > 1:
            up[...] = total
        else:
            own[d] = total

    after, before = lax.rem(z + 1, slabs), lax.rem(z + slabs - 1, slabs)

    def rims(i, block_up, block_down, from_below, from_above):
        return (
            remote(block_up, from_below, hs.at[i], hr.at[i], "slab", after),
            remote(block_down, from_above, hs.at[i + 1], hr.at[i + 1], "slab", before),
        )

    first_rims = rims(0, up, down, below, above)
    for copy in first_rims:
        copy.start()
    inside = (z > 0, z < slabs - 1)
    for copy in first_rims:
        copy.wait_recv()
    for d in range(2):
        rim = (below if d == 0 else above)[...]
        second_pre = own[d] + jnp.where(inside[d], rim, 0.0)
        result_ref[:, d] = silu_value(second_pre).astype(BF)
        grad = og_ref[:, d].astype(F32) * silu_slope(second_pre)
        sg[d] = grad.astype(BF)
    second_rims = rims(2, sg.at[1], sg.at[0], sg_below, sg_above)
    for copy in second_rims:
        copy.start()

    def put_view(plane, values):
        for g in range(3):
            view[g, :, plane + 1, 1:5] = shifted(values, 1 - g)

    for d in range(2):
        put_view(d, sg[d].astype(F32))
    for copy in second_rims:
        copy.wait_recv()
    put_view(-1, jnp.where(inside[0], sg_below[...].astype(F32), 0.0))
    put_view(2, jnp.where(inside[1], sg_above[...].astype(F32), 0.0))
    for d in range(2):
        for a in range(3):
            for e in range(3):
                for g in range(3):
                    at = tap(a, e, g)
                    s[:, d, :, at : at + 8, :] = view[g, :, d - a + 2, 2 - e : 6 - e]

    def back(q, total):
        b, d, h = lax.div(q, 8), lax.rem(lax.div(q, 4), 2), lax.rem(q, 4)
        taps = s[b, d, h].astype(BF)
        mid[q] = jnp.dot(w2_t[...], taps, preferred_element_type=F32).astype(BF)
        return total + nt_dot(taps, hid[q])

    total = lax.fori_loop(0, 16, back, jnp.zeros((216, 128), F32))
    to_all(lambda r: filt(3, r, mid.at[peer(r)], mid_in.at[f]).start())
    two[:TAPS] = total.reshape(TAPS, 8, 128)
    two_sums = Scatter(
        slabs, z, 0, two_count, two, two_in, two_sum, two_out, (ts_a, tr_a, ts_b, tr_b)
    )
    two_sums.start()

    def get_mid(r, total):
        filt(3, r, mid.at[peer(r)], mid_in.at[source(r)]).wait_recv()
        return total + mid_in[source(r)].astype(F32)

    mid_grad = lax.fori_loop(1, filts, get_mid, mid[f].astype(F32))
    grad = (mid_grad * silu_slope(pre_ref[...])).astype(BF)
    x = x_all[...].reshape(256, 256)
    for k in range(2):
        part = nt_dot(grad, x[:, k * 128 : (k + 1) * 128])
        dw1[:, :, k * 256 : (k + 1) * 256] = part.reshape(16, 8, 256)
    to_all(lambda r: filt(4, r, dw1.at[peer(r)], dw1_in.at[f]).start())
    two_sums.reduce()

    def get_one(r, total):
        filt(4, r, dw1.at[peer(r)], dw1_in.at[source(r)]).wait_recv()
        return total + dw1_in[source(r)]

    first = lax.fori_loop(1, filts, get_one, dw1[f])
    for j in range(W1_BLOCKS):
        one[j] = first[:, j * 128 : (j + 1) * 128]
    one_first = TAPS if slabs >= TAPS + W1_BLOCKS else 0
    one_sums = Scatter(
        slabs, z, one_first, one_count, one, one_in, one_sum, one_out,
        (os_a, or_a, os_b, or_b),
    )
    one_sums.start()
    one_sums.reduce()
    two_sums.finish()
    one_sums.finish()

    def sent(r):
        filt(0, r, piece.at[peer(r)], x_all.at[f]).wait_send()
        filt(1, r, w1_ref, w_all.at[f]).wait_send()
        filt(2, r, hid.at[f], hid.at[f]).wait_send()
        filt(3, r, mid.at[peer(r)], mid_in.at[f]).wait_send()
        filt(4, r, dw1.at[peer(r)], dw1_in.at[f]).wait_send()

    to_all(sent)
    for copy in first_rims + second_rims:
        copy.wait_send()


def owners(blocks, n):
    per = -(-blocks // n)
    return -(-blocks // per), per


def level(x, w1, w2, og):
    filts, slabs = lax.axis_size("filt"), lax.axis_size("slab")
    two_count, one_count = owners(TAPS, slabs), owners(W1_BLOCKS, slabs)
    two_size, one_size = (c[0] * c[1] for c in (two_count, one_count))
    sem = pltpu.SemaphoreType.DMA
    buffers = [
        ((16, 16, 256), BF), ((16, 16, 256), BF), ((16, 8, 512), BF),
        ((16, 128, 128), BF), ((2, 2, 6, 216, 128), F32), ((2, 2, 4, 8, 128), F32),
        ((2, 4, 8, 128), F32), ((2, 4, 8, 128), F32),
        ((2, 4, 8, 128), F32), ((2, 4, 8, 128), F32),
        ((2, 2, 4, 8, 128), BF), ((2, 4, 8, 128), BF), ((2, 4, 8, 128), BF),
        ((3, 2, 4, 6, 8, 128), F32), ((2, 2, 4, 216, 128), F32),
        ((16, 128, 128), BF), ((16, 128, 128), BF),
        ((16, 8, 512), F32), ((16, 8, 512), F32), ((128, 216), BF), ((128, 128), F32),
        ((two_size, 8, 128), F32), ((slabs, two_count[1], 8, 128), F32),
        ((two_count[1], 8, 128), F32),
        ((one_size, 8, 128), F32), ((slabs, one_count[1], 8, 128), F32),
        ((one_count[1], 8, 128), F32),
    ]
    return pl.pallas_call(
        functools.partial(level_kernel, filts, slabs, two_count, one_count),
        out_shape=[
            jax.ShapeDtypeStruct((2, 2, 4, 8, 128), BF),
            jax.ShapeDtypeStruct((two_size, 8, 128), F32),
            jax.ShapeDtypeStruct((one_size, 8, 128), F32),
        ],
        in_specs=[VMEM] * 4,
        out_specs=[VMEM] * 3,
        scratch_shapes=[pltpu.VMEM(shape, dtype) for shape, dtype in buffers]
        + [
            sem((5, filts)), sem((5, filts)), sem((4,)), sem((4,)),
            sem((two_count[0],)), sem((slabs,)), sem((slabs,)), sem((two_count[0],)),
            sem((one_count[0],)), sem((slabs,)), sem((slabs,)), sem((one_count[0],)),
        ],
        compiler_params=pltpu.CompilerParams(collective_id=1, has_side_effects=True),
        name="level",
    )(x, w1, w2, og)


def on_device(volume, first_weight, second_weight, out_grad):
    w1 = first_weight.transpose(1, 4, 0, 2, 3).reshape(8, 512)
    w2 = second_weight.transpose(2, 3, 4, 1, 0).reshape(216, 128)
    og = out_grad.transpose(0, 2, 3, 1, 4)
    result, two, one = level(volume.reshape(256, 256), w1, w2, og)
    weight_two = two[:TAPS].reshape(3, 3, 3, 8, 128).transpose(4, 3, 0, 1, 2)
    one = one.reshape(2, 2, 8, 32, 2, 2).transpose(1, 3, 2, 4, 5, 0)
    weight_one = one.reshape(64, 8, 2, 2, 2)
    return (result.transpose(0, 3, 1, 2, 4), weight_one, weight_two)


def solution(mesh):
    in_specs = (
        P(None, "filt", "slab", None, None),
        P(None, "filt", None, None, None),
        P(None, "filt", None, None, None),
        P(None, "filt", "slab", None, None),
    )
    out_specs = (
        P(None, "filt", "slab", None, None),
        P(None, "filt", None, None, None),
        P(None, "filt", None, None, None),
    )
    return jax.shard_map(
        on_device, mesh=mesh, in_specs=in_specs, out_specs=out_specs, check_vma=False
    )
```

time: 763 us -> 99.6 us (0.13)
  waiting for transfers between devices: 454 us -> 0 us
  blocking collectives: 164 us -> 0 us
  Pallas kernels: 0 us -> 93.4 us
  matrix products: 45.8 us -> 0 us
  local copies, waits for them, and re-layouts: 44.6 us -> 5.25 us
  starting transfers between devices: 23.7 us -> 0 us
  between operations: 14.8 us -> 0.68 us
  other arithmetic: 13.7 us -> 0 us
    all_gather x2 -> x0, waiting for transfers between devices: 196 us -> none  [the longest x1 110 us: on_device(): all_inputs = lax.all_gather(extended, 'filt', axis=1, tiled=True)]
    psum x1 -> x0, blocking collectives: 164 us -> none  [on_device(): weight_one, weight_two = lax.psum((weight_one, weight_two), 'slab')]
    unnamed x5 -> x0, waiting for transfers between devices: 129 us -> none
    psum x1 -> x0, waiting for transfers between devices: 126 us -> none  [on_device(): weight_one, weight_two = lax.psum((weight_one, weight_two), 'slab')]
    pallas_call x0 -> x1, Pallas kernels: none -> 93.4 us  [level(): pl.pallas_call(functools.partial(level_kernel, filts, slabs, two_count, o...]
    conv_general_dilated x5 -> x0, matrix products: 45.8 us -> none  [the longest x1 16.2 us: on_device(): lax.conv_general_dilated(hidden_pad, second_weight, (1, 1, 1), 'VALID', d...]
    all_gather x4 -> x0, local copies, waits for them, and re-layouts: 26.1 us -> none  [the longest x2 24 us: on_device(): all_inputs = lax.all_gather(extended, 'filt', axis=1, tiled=True)]
    ppermute x4 -> x0, starting transfers between devices: 23.3 us -> none  [the longest x2 13.1 us: padded(): before = lax.ppermute(last, axis, up)]
  transfers between devices with their start and end apart: 8 -> 0, of which waited for: 6 -> 0; matrix products, arithmetic and copies ran while one was open for 5% -> 0% of each run, Pallas kernels for 0% -> 0%
where the time goes in v2:
time: 99.6 us; the launch traced here: 99.3 us
  Pallas kernels  93.4 us (94%)
  local copies, waits for them, and re-layouts  5.25 us (5%)
    pallas_call x1, Pallas kernels, level(): pl.pallas_call(functools.partial(level_kernel, filts, slabs, two_count, o...  93.4 us
    unnamed x10, local copies, waits for them, and re-layouts  4.32 us

profile of v2, /device:TPU:1, one launch (start us, length us, event | category | flops | bytes accessed | tf_op | source)
XLA Modules:
  0.0 99.3 jit_solution(2315297503717659342)
XLA Ops:
  0.6 0.0 copy-start.1
  0.6 1.4 %copy.18 = bf16[2,8,2,4,128]{4,1,3,2,0:T(8,128)(2,1)} copy(bf16[2,8,2,4,128]{4,3,2,1,0:T(4,128)(2,1)} %param.7) | data formatting | bytes 65536 | tf_op args[3]
  2.0 0.0 copy-done.1
  2.0 0.1 copy.11
  2.2 0.7 copy.13.w1_ref
  2.8 93.4 %level.1 = (bf16[2,2,4,8,128]{4,3,2,1,0:T(8,128)(2,1)}, f32[27,8,128]{2,1,0:T(8,128)}, f32[4,8,128]{2,1,0:T(8,128)}) custom-call(bf16[256,256]{1,0:T(8,128)(2,1)} %bitcast.20, bf16[8,512]{1,0:T(8,128)(2,1)} %copy.13.w1_ref, bf16[216,128]{1,0:T(8,128)(2,1)} %bitcast.23, bf16[2,2,4,8,128]{4,3,2,1,0:T(8,128)(2,1)} %bitcast.21), custom_call_target="tpu_custom_call" | custom-call | tf_op jit(solution)/shard_map/level/pallas_call | solution.py:390
  96.2 0.0 copy-start.2
  96.3 1.4 %copy.15 = bf16[2,8,2,4,128]{4,3,2,1,0:T(4,128)(2,1)} copy(bf16[2,8,2,4,128]{4,1,3,2,0:T(8,128)(2,1)} %bitcast.24) | data formatting | bytes 65536
  97.6 0.0 copy-done.2
  97.7 0.1 copy.14
  97.8 0.0 copy-start
  97.8 0.8 copy.16
  98.6 0.1 copy-done
  98.7 0.6 copy.20
Async XLA Ops:
  0.6 1.4 %copy-start.1 = (bf16[64,8,2,2,2]{0,4,3,2,1:T(2,128)(2,1)S(1)}, bf16[64,8,2,2,2]{0,4,3,2,1:T(2,128)(2,1)}, u32[]{:S(2)}) copy-start(bf16[64,8,2,2,2]{0,4,3,2,1:T(2,128)(2,1)} %param.5) | copy-start | bytes 24580
  96.2 1.4 %copy-start.2 = (f32[4,8,128]{2,1,0:T(8,128)S(1)}, f32[4,8,128]{2,1,0:T(8,128)}, u32[]{:S(2)}) copy-start(f32[4,8,128]{2,1,0:T(8,128)} %get-tuple-element.7) | copy-start | bytes 49156
  97.8 0.9 copy-start

commit v3 on v2

--- a/solution.py
+++ b/solution.py
@@ -72,6 +72,85 @@
 
 def repeat(low, high, step):
     lax.fori_loop(low, high, lambda i, carry: (step(i), carry)[1], 0)
+
+
+class Ring:
+    def __init__(self, f, buffer, send, recv):
+        self.column, self.y = lax.div(f, 8), lax.rem(f, 8)
+        self.buffer, self.send, self.recv = buffer, send, recv
+
+    def device(self, c, y):
+        return lax.rem(self.column + c, 2) * 8 + lax.rem(y + 8, 8)
+
+    def piece(self, c, way, h):
+        return self.device(c, self.y - h if way == 0 else self.y + h)
+
+    def hop(self, c, way, h):
+        block = self.buffer.at[self.piece(c, way, h - 1)]
+        to = self.device(0, self.y + 1 if way == 0 else self.y - 1)
+        at = c * 2 + way
+        return remote(
+            block, block, self.send.at[at, h], self.recv.at[at, h], "filt", to
+        )
+
+    def cross(self):
+        block = self.buffer.at[self.device(0, self.y)]
+        return remote(
+            block, block, self.send.at[0, 0], self.recv.at[0, 0],
+            "filt", self.device(1, self.y),
+        )
+
+    def landed(self, c, way, h):
+        block = self.buffer.at[self.piece(c, way, h)]
+        at = c * 2 + way
+        remote(
+            block, block, self.send.at[at, h], self.recv.at[at, h],
+            "filt", self.device(0, self.y),
+        ).wait_recv()
+
+    def run(self, use):
+        self.cross().start()
+        self.hop(0, 0, 1).start()
+        self.hop(0, 1, 1).start()
+        use(self.piece(0, 0, 0))
+        partner = self.buffer.at[self.device(1, self.y)]
+        remote(
+            partner, partner, self.send.at[0, 0], self.recv.at[0, 0],
+            "filt", self.device(1, self.y),
+        ).wait_recv()
+        self.hop(1, 0, 1).start()
+        self.hop(1, 1, 1).start()
+        use(self.piece(1, 0, 0))
+
+        def step(h):
+            for c in range(2):
+                self.landed(c, 0, h)
+                self.hop(c, 0, h + 1).start()
+                self.landed(c, 1, h)
+
+                @pl.when(h < 3)
+                def _():
+                    self.hop(c, 1, h + 1).start()
+
+                use(self.piece(c, 0, h))
+                use(self.piece(c, 1, h))
+
+        repeat(1, 4, step)
+        for c in range(2):
+            self.landed(c, 0, 4)
+            use(self.piece(c, 0, 4))
+
+    def sent(self):
+        self.cross().wait_send()
+
+        def step(h):
+            for c in range(2):
+                self.hop(c, 0, h).wait_send()
+                self.hop(c, 1, h).wait_send()
+
+        repeat(1, 4, step)
+        for c in range(2):
+            self.hop(c, 0, 4).wait_send()
 
 
 class Scatter:
@@ -170,7 +249,7 @@
     piece, x_all, w_all, hid, y, own, up, down, below, above,
     sg, sg_below, sg_above, view, s, mid, mid_in, dw1, dw1_in, w2_t, pre_ref,
     two, two_in, two_sum, one, one_in, one_sum,
-    fs, fr, hs, hr, ts_a, tr_a, ts_b, tr_b, os_a, or_a, os_b, or_b,
+    og, res, fs, fr, gs, gr, hs, hr, ts_a, tr_a, ts_b, tr_b, os_a, or_a, os_b, or_b,
 ):
     f, z = lax.axis_index("filt"), lax.axis_index("slab")
     barrier = pltpu.get_barrier_semaphore()
@@ -214,6 +293,10 @@
         filt(1, r, w1_ref, w_all.at[f]).start()
 
     to_all(send_x)
+    for b in range(2):
+        for d in range(2):
+            for n in range(8):
+                og[d, b, :, n, :] = og_ref[b, n, d].astype(F32)
     eye = one_hot(lambda o: o, 128)
     w2_t[...] = nt_dot(eye, w2_ref[...]).astype(BF)
     y[:, :, 0] = jnp.zeros((2, 2, 216, 128), F32)
@@ -232,19 +315,13 @@
     pre += jnp.dot(w[:, 256:], x[:, 128:], preferred_element_type=F32)
     pre_ref[...] = pre
     hid[f] = silu_value(pre).astype(BF)
-    to_all(lambda r: filt(2, r, hid.at[f], hid.at[f]).start())
 
     def spread(q):
         b, d, h = lax.div(q, 8), lax.rem(lax.div(q, 4), 2), lax.rem(q, 4)
         y[b, d, h + 1] = jnp.dot(w2_ref[...], hid[q], preferred_element_type=F32)
 
-    spread(f)
-
-    def get_hidden(r):
-        filt(2, r, hid.at[f], hid.at[source(r)]).wait_recv()
-        spread(source(r))
-
-    to_all(get_hidden)
+    ring = Ring(f, hid, gs, gr)
+    ring.run(spread)
     for d in (-1, 2, 0, 1):
         total = None
         for g in range(3):
@@ -283,8 +360,8 @@
     for d in range(2):
         rim = (below if d == 0 else above)[...]
         second_pre = own[d] + jnp.where(inside[d], rim, 0.0)
-        result_ref[:, d] = silu_value(second_pre).astype(BF)
-        grad = og_ref[:, d].astype(F32) * silu_slope(second_pre)
+        res[d] = silu_value(second_pre)
+        grad = og[d] * silu_slope(second_pre)
         sg[d] = grad.astype(BF)
     second_rims = rims(2, sg.at[1], sg.at[0], sg_below, sg_above)
     for copy in second_rims:
@@ -296,6 +373,9 @@
 
     for d in range(2):
         put_view(d, sg[d].astype(F32))
+        for b in range(2):
+            for n in range(8):
+                result_ref[b, n, d] = res[d, b, :, n, :].astype(BF)
     for copy in second_rims:
         copy.wait_recv()
     put_view(-1, jnp.where(inside[0], sg_below[...].astype(F32), 0.0))
@@ -354,11 +434,11 @@
     def sent(r):
         filt(0, r, piece.at[peer(r)], x_all.at[f]).wait_send()
         filt(1, r, w1_ref, w_all.at[f]).wait_send()
-        filt(2, r, hid.at[f], hid.at[f]).wait_send()
         filt(3, r, mid.at[peer(r)], mid_in.at[f]).wait_send()
         filt(4, r, dw1.at[peer(r)], dw1_in.at[f]).wait_send()
 
     to_all(sent)
+    ring.sent()
     for copy in first_rims + second_rims:
         copy.wait_send()
 
@@ -386,11 +466,12 @@
         ((two_count[1], 8, 128), F32),
         ((one_size, 8, 128), F32), ((slabs, one_count[1], 8, 128), F32),
         ((one_count[1], 8, 128), F32),
+        ((2, 2, 4, 8, 128), F32), ((2, 2, 4, 8, 128), F32),
     ]
     return pl.pallas_call(
         functools.partial(level_kernel, filts, slabs, two_count, one_count),
         out_shape=[
-            jax.ShapeDtypeStruct((2, 2, 4, 8, 128), BF),
+            jax.ShapeDtypeStruct((2, 8, 2, 4, 128), BF),
             jax.ShapeDtypeStruct((two_size, 8, 128), F32),
             jax.ShapeDtypeStruct((one_size, 8, 128), F32),
         ],
@@ -398,7 +479,7 @@
         out_specs=[VMEM] * 3,
         scratch_shapes=[pltpu.VMEM(shape, dtype) for shape, dtype in buffers]
         + [
-            sem((5, filts)), sem((5, filts)), sem((4,)), sem((4,)),
+            sem((5, filts)), sem((5, filts)), sem((4, 5)), sem((4, 5)), sem((4,)), sem((4,)),
             sem((two_count[0],)), sem((slabs,)), sem((slabs,)), sem((two_count[0],)),
             sem((one_count[0],)), sem((slabs,)), sem((slabs,)), sem((one_count[0],)),
         ],
@@ -410,12 +491,11 @@
 def on_device(volume, first_weight, second_weight, out_grad):
     w1 = first_weight.transpose(1, 4, 0, 2, 3).reshape(8, 512)
     w2 = second_weight.transpose(2, 3, 4, 1, 0).reshape(216, 128)
-    og = out_grad.transpose(0, 2, 3, 1, 4)
-    result, two, one = level(volume.reshape(256, 256), w1, w2, og)
+    result, two, one = level(volume.reshape(256, 256), w1, w2, out_grad)
     weight_two = two[:TAPS].reshape(3, 3, 3, 8, 128).transpose(4, 3, 0, 1, 2)
     one = one.reshape(2, 2, 8, 32, 2, 2).transpose(1, 3, 2, 4, 5, 0)
     weight_one = one.reshape(64, 8, 2, 2, 2)
-    return (result.transpose(0, 3, 1, 2, 4), weight_one, weight_two)
+    return (result, weight_one, weight_two)
 
 
 def solution(mesh):

time: 99.6 us -> 102 us (1.024)
  Pallas kernels: 93.4 us -> 96.3 us
    pallas_call x1, Pallas kernels: 93.4 us -> 96.3 us  [level(): pl.pallas_call(functools.partial(level_kernel, filts, slabs, two_count, o...]
    unnamed x10 -> x7, local copies, waits for them, and re-layouts: 4.32 us -> 2.07 us
where the time goes in v3:
time: 102 us; the launch traced here: 101 us
  Pallas kernels  96.3 us (94%)
  local copies, waits for them, and re-layouts  4.46 us (4%)
    pallas_call x1, Pallas kernels, level(): pl.pallas_call(functools.partial(level_kernel, filts, slabs, two_count, o...  96.3 us
    unnamed x7, local copies, waits for them, and re-layouts  2.07 us

profile of v3, /device:TPU:1, one launch (start us, length us, event | category | flops | bytes accessed | tf_op | source)
XLA Modules:
  0.0 101.4 jit_solution(10143594634789403028)
XLA Ops:
  0.6 0.9 copy.9
  1.5 0.7 copy.10.w1_ref
  2.2 96.3 %level.1 = (bf16[2,8,2,4,128]{4,3,2,1,0:T(4,128)(2,1)}, f32[27,8,128]{2,1,0:T(8,128)}, f32[4,8,128]{2,1,0:T(8,128)}) custom-call(bf16[256,256]{1,0:T(8,128)(2,1)} %bitcast.16, bf16[8,512]{1,0:T(8,128)(2,1)} %copy.10.w1_ref, bf16[216,128]{1,0:T(8,128)(2,1)} %bitcast.18, bf16[2,8,2,4,128]{4,3,2,1,0:T(4,128)(2,1)} %og_ref.1), custom_call_target="tpu_custom_call" | custom-call | tf_op jit(solution)/shard_map/level/pallas_call | solution.py:471
  98.5 0.8 copy.11
  99.3 0.0 copy-start.1
  99.3 0.0 copy-start
  99.4 0.8 copy.12
  100.2 0.0 copy-done.1
  100.2 0.6 copy.15
  100.8 0.0 copy-done
  100.8 0.6 copy.16
Async XLA Ops:
  99.3 0.8 copy-start.1
  99.3 1.4 %copy-start = (f32[27,8,128]{2,1,0:T(8,128)S(1)}, f32[27,8,128]{2,1,0:T(8,128)}, u32[]{:S(2)}) copy-start(f32[27,8,128]{2,1,0:T(8,128)} %get-tuple-element.8) | copy-start | bytes 331780

commit v4 on v2

--- a/solution.py
+++ b/solution.py
@@ -170,7 +170,7 @@
     piece, x_all, w_all, hid, y, own, up, down, below, above,
     sg, sg_below, sg_above, view, s, mid, mid_in, dw1, dw1_in, w2_t, pre_ref,
     two, two_in, two_sum, one, one_in, one_sum,
-    fs, fr, hs, hr, ts_a, tr_a, ts_b, tr_b, os_a, or_a, os_b, or_b,
+    og, res, fs, fr, hs, hr, ts_a, tr_a, ts_b, tr_b, os_a, or_a, os_b, or_b,
 ):
     f, z = lax.axis_index("filt"), lax.axis_index("slab")
     barrier = pltpu.get_barrier_semaphore()
@@ -189,17 +189,28 @@
     greet("filt", f, filts)
     greet("slab", z, slabs)
 
+    def other(r, sign):
+        m = lax.div(r, 2)
+        dy = 4 + (1 - 2 * lax.rem(m, 2)) * lax.div(m + 1, 2)
+        column = lax.rem(lax.div(f, 8) + 1 + lax.rem(r, 2), 2)
+        return column * 8 + lax.rem(lax.rem(f, 8) + 8 + sign * dy, 8)
+
     def peer(r):
-        return lax.rem(f + r, filts)
+        return other(r, 1)
 
     def source(r):
-        return lax.rem(f + filts - r, filts)
+        return other(r, -1)
 
     def filt(i, r, block, target):
         return remote(block, target, fs.at[i, r], fr.at[i, r], "filt", peer(r))
 
     def to_all(step):
-        repeat(1, filts, step)
+        repeat(0, filts - 1, step)
+
+    def from_all(step, start):
+        return lax.fori_loop(
+            0, filts - 1, lambda r, carry: step(filts - 2 - r, carry), start
+        )
 
     rows, columns = piece_matrices()
     half = jnp.dot(rows, x_ref[...], preferred_element_type=F32).astype(BF)
@@ -214,6 +225,10 @@
         filt(1, r, w1_ref, w_all.at[f]).start()
 
     to_all(send_x)
+    for b in range(2):
+        for d in range(2):
+            for n in range(8):
+                og[d, b, :, n, :] = og_ref[b, n, d].astype(F32)
     eye = one_hot(lambda o: o, 128)
     w2_t[...] = nt_dot(eye, w2_ref[...]).astype(BF)
     y[:, :, 0] = jnp.zeros((2, 2, 216, 128), F32)
@@ -244,7 +259,7 @@
         filt(2, r, hid.at[f], hid.at[source(r)]).wait_recv()
         spread(source(r))
 
-    to_all(get_hidden)
+    from_all(lambda r, carry: (get_hidden(r), carry)[1], 0)
     for d in (-1, 2, 0, 1):
         total = None
         for g in range(3):
@@ -283,8 +298,8 @@
     for d in range(2):
         rim = (below if d == 0 else above)[...]
         second_pre = own[d] + jnp.where(inside[d], rim, 0.0)
-        result_ref[:, d] = silu_value(second_pre).astype(BF)
-        grad = og_ref[:, d].astype(F32) * silu_slope(second_pre)
+        res[d] = silu_value(second_pre)
+        grad = og[d] * silu_slope(second_pre)
         sg[d] = grad.astype(BF)
     second_rims = rims(2, sg.at[1], sg.at[0], sg_below, sg_above)
     for copy in second_rims:
@@ -296,25 +311,52 @@
 
     for d in range(2):
         put_view(d, sg[d].astype(F32))
+        for b in range(2):
+            for n in range(8):
+                result_ref[b, n, d] = res[d, b, :, n, :].astype(BF)
+
+    def put_taps(d, a):
+        for e in range(3):
+            for g in range(3):
+                at = tap(a, e, g)
+                s[:, d, :, at : at + 8, :] = view[g, :, d - a + 2, 2 - e : 6 - e]
+
+    for d in range(2):
+        put_taps(d, 1)
+        put_taps(d, 2 * d)
     for copy in second_rims:
         copy.wait_recv()
     put_view(-1, jnp.where(inside[0], sg_below[...].astype(F32), 0.0))
     put_view(2, jnp.where(inside[1], sg_above[...].astype(F32), 0.0))
     for d in range(2):
-        for a in range(3):
-            for e in range(3):
-                for g in range(3):
-                    at = tap(a, e, g)
-                    s[:, d, :, at : at + 8, :] = view[g, :, d - a + 2, 2 - e : 6 - e]
-
-    def back(q, total):
+        put_taps(d, 2 - 2 * d)
+
+    def taps_of(q):
         b, d, h = lax.div(q, 8), lax.rem(lax.div(q, 4), 2), lax.rem(q, 4)
-        taps = s[b, d, h].astype(BF)
-        mid[q] = jnp.dot(w2_t[...], taps, preferred_element_type=F32).astype(BF)
-        return total + nt_dot(taps, hid[q])
-
-    total = lax.fori_loop(0, 16, back, jnp.zeros((216, 128), F32))
-    to_all(lambda r: filt(3, r, mid.at[peer(r)], mid_in.at[f]).start())
+        return s[b, d, h].astype(BF)
+
+    def back(q):
+        part = jnp.dot(w2_t[...], taps_of(q), preferred_element_type=F32)
+        mid[q] = part.astype(BF)
+
+    def send_mid(r):
+        filt(3, r, mid.at[peer(r)], mid_in.at[f]).start()
+
+    back(peer(0))
+
+    def back_step(r):
+        back(peer(r))
+        send_mid(r - 1)
+
+    repeat(1, filts - 1, back_step)
+    back(f)
+    send_mid(filts - 2)
+    total = lax.fori_loop(
+        0,
+        filts,
+        lambda q, total: total + nt_dot(taps_of(q), hid[q]),
+        jnp.zeros((216, 128), F32),
+    )
     two[:TAPS] = total.reshape(TAPS, 8, 128)
     two_sums = Scatter(
         slabs, z, 0, two_count, two, two_in, two_sum, two_out, (ts_a, tr_a, ts_b, tr_b)
@@ -325,7 +367,7 @@
         filt(3, r, mid.at[peer(r)], mid_in.at[source(r)]).wait_recv()
         return total + mid_in[source(r)].astype(F32)
 
-    mid_grad = lax.fori_loop(1, filts, get_mid, mid[f].astype(F32))
+    mid_grad = from_all(get_mid, mid[f].astype(F32))
     grad = (mid_grad * silu_slope(pre_ref[...])).astype(BF)
     x = x_all[...].reshape(256, 256)
     for k in range(2):
@@ -338,7 +380,7 @@
         filt(4, r, dw1.at[peer(r)], dw1_in.at[source(r)]).wait_recv()
         return total + dw1_in[source(r)]
 
-    first = lax.fori_loop(1, filts, get_one, dw1[f])
+    first = from_all(get_one, dw1[f])
     for j in range(W1_BLOCKS):
         one[j] = first[:, j * 128 : (j + 1) * 128]
     one_first = TAPS if slabs >= TAPS + W1_BLOCKS else 0
@@ -347,9 +389,6 @@
         (os_a, or_a, os_b, or_b),
     )
     one_sums.start()
-    one_sums.reduce()
-    two_sums.finish()
-    one_sums.finish()
 
     def sent(r):
         filt(0, r, piece.at[peer(r)], x_all.at[f]).wait_send()
@@ -361,6 +400,9 @@
     to_all(sent)
     for copy in first_rims + second_rims:
         copy.wait_send()
+    one_sums.reduce()
+    two_sums.finish()
+    one_sums.finish()
 
 
 def owners(blocks, n):
@@ -386,11 +428,12 @@
         ((two_count[1], 8, 128), F32),
         ((one_size, 8, 128), F32), ((slabs, one_count[1], 8, 128), F32),
         ((one_count[1], 8, 128), F32),
+        ((2, 2, 4, 8, 128), F32), ((2, 2, 4, 8, 128), F32),
     ]
     return pl.pallas_call(
         functools.partial(level_kernel, filts, slabs, two_count, one_count),
         out_shape=[
-            jax.ShapeDtypeStruct((2, 2, 4, 8, 128), BF),
+            jax.ShapeDtypeStruct((2, 8, 2, 4, 128), BF),
             jax.ShapeDtypeStruct((two_size, 8, 128), F32),
             jax.ShapeDtypeStruct((one_size, 8, 128), F32),
         ],
@@ -410,12 +453,11 @@
 def on_device(volume, first_weight, second_weight, out_grad):
     w1 = first_weight.transpose(1, 4, 0, 2, 3).reshape(8, 512)
     w2 = second_weight.transpose(2, 3, 4, 1, 0).reshape(216, 128)
-    og = out_grad.transpose(0, 2, 3, 1, 4)
-    result, two, one = level(volume.reshape(256, 256), w1, w2, og)
+    result, two, one = level(volume.reshape(256, 256), w1, w2, out_grad)
     weight_two = two[:TAPS].reshape(3, 3, 3, 8, 128).transpose(4, 3, 0, 1, 2)
     one = one.reshape(2, 2, 8, 32, 2, 2).transpose(1, 3, 2, 4, 5, 0)
     weight_one = one.reshape(64, 8, 2, 2, 2)
-    return (result.transpose(0, 3, 1, 2, 4), weight_one, weight_two)
+    return (result, weight_one, weight_two)
 
 
 def solution(mesh):

time: 99.6 us -> 96.1 us (0.965)
  Pallas kernels: 93.4 us -> 90.6 us
    pallas_call x1, Pallas kernels: 93.4 us -> 90.6 us  [level(): pl.pallas_call(functools.partial(level_kernel, filts, slabs, two_count, o...]
    unnamed x10 -> x7, local copies, waits for them, and re-layouts: 4.32 us -> 2.07 us
where the time goes in v4:
time: 96.1 us; the launch traced here: 95.7 us
  Pallas kernels  90.6 us (94%)
  local copies, waits for them, and re-layouts  4.46 us (5%)
    pallas_call x1, Pallas kernels, level(): pl.pallas_call(functools.partial(level_kernel, filts, slabs, two_count, o...  90.6 us
    unnamed x7, local copies, waits for them, and re-layouts  2.07 us

profile of v4, /device:TPU:1, one launch (start us, length us, event | category | flops | bytes accessed | tf_op | source)
XLA Modules:
  0.0 95.7 jit_solution(11685068297055459712)
XLA Ops:
  0.6 0.9 copy.9
  1.5 0.7 copy.10.w1_ref
  2.2 90.6 %level.1 = (bf16[2,8,2,4,128]{4,3,2,1,0:T(4,128)(2,1)}, f32[27,8,128]{2,1,0:T(8,128)}, f32[4,8,128]{2,1,0:T(8,128)}) custom-call(bf16[256,256]{1,0:T(8,128)(2,1)} %bitcast.16, bf16[8,512]{1,0:T(8,128)(2,1)} %copy.10.w1_ref, bf16[216,128]{1,0:T(8,128)(2,1)} %bitcast.18, bf16[2,8,2,4,128]{4,3,2,1,0:T(4,128)(2,1)} %og_ref.1), custom_call_target="tpu_custom_call" | custom-call | tf_op jit(solution)/shard_map/level/pallas_call | solution.py:433
  92.8 0.8 copy.11
  93.7 0.0 copy-start.1
  93.7 0.0 copy-start
  93.7 0.8 copy.12
  94.5 0.0 copy-done.1
  94.5 0.6 copy.15
  95.1 0.0 copy-done
  95.1 0.6 copy.16
Async XLA Ops:
  93.7 0.8 copy-start.1
  93.7 1.4 %copy-start = (f32[27,8,128]{2,1,0:T(8,128)S(1)}, f32[27,8,128]{2,1,0:T(8,128)}, u32[]{:S(2)}) copy-start(f32[27,8,128]{2,1,0:T(8,128)} %get-tuple-element.8) | copy-start | bytes 331780

commit v5 on v4

--- a/solution.py
+++ b/solution.py
@@ -11,6 +11,7 @@
 F32 = jnp.float32
 MESH = pl.DeviceIdType.MESH
 VMEM = pl.BlockSpec(memory_space=pltpu.VMEM)
+ANY = pl.BlockSpec(memory_space=pl.ANY)
 TAPS = 27
 W1_BLOCKS = 4
 
@@ -165,15 +166,23 @@
 
 def level_kernel(
     filts, slabs, two_count, one_count,
-    x_ref, w1_ref, w2_ref, og_ref,
-    result_ref, two_out, one_out,
+    x_hbm, w1_ref, w2_hbm, og_hbm,
+    result_hbm, two_out, one_out,
     piece, x_all, w_all, hid, y, own, up, down, below, above,
     sg, sg_below, sg_above, view, s, mid, mid_in, dw1, dw1_in, w2_t, pre_ref,
     two, two_in, two_sum, one, one_in, one_sum,
-    og, res, fs, fr, hs, hr, ts_a, tr_a, ts_b, tr_b, os_a, or_a, os_b, or_b,
+    og, res, x_ref, w2_ref, og_ref, result_ref, ls, fs, fr, hs, hr, ts_a, tr_a, ts_b, tr_b, os_a, or_a, os_b, or_b,
 ):
     f, z = lax.axis_index("filt"), lax.axis_index("slab")
     barrier = pltpu.get_barrier_semaphore()
+    loads = [
+        pltpu.make_async_copy(array, place, ls.at[i])
+        for i, (array, place) in enumerate(
+            ((x_hbm, x_ref), (w2_hbm, w2_ref), (og_hbm, og_ref))
+        )
+    ]
+    for copy in loads:
+        copy.start()
 
     def greet(axis, me, n):
         def one_peer(r):
@@ -213,6 +222,7 @@
         )
 
     rows, columns = piece_matrices()
+    loads[0].wait()
     half = jnp.dot(rows, x_ref[...], preferred_element_type=F32).astype(BF)
     cut = jnp.dot(half, columns, preferred_element_type=F32).astype(BF)
     piece[...] = cut.reshape(piece.shape)
@@ -225,6 +235,8 @@
         filt(1, r, w1_ref, w_all.at[f]).start()
 
     to_all(send_x)
+    loads[1].wait()
+    loads[2].wait()
     for b in range(2):
         for d in range(2):
             for n in range(8):
@@ -357,6 +369,8 @@
         lambda q, total: total + nt_dot(taps_of(q), hid[q]),
         jnp.zeros((216, 128), F32),
     )
+    store = pltpu.make_async_copy(result_ref, result_hbm, ls.at[3])
+    store.start()
     two[:TAPS] = total.reshape(TAPS, 8, 128)
     two_sums = Scatter(
         slabs, z, 0, two_count, two, two_in, two_sum, two_out, (ts_a, tr_a, ts_b, tr_b)
@@ -372,15 +386,15 @@
     x = x_all[...].reshape(256, 256)
     for k in range(2):
         part = nt_dot(grad, x[:, k * 128 : (k + 1) * 128])
-        dw1[:, :, k * 256 : (k + 1) * 256] = part.reshape(16, 8, 256)
+        dw1[:, :, k * 256 : (k + 1) * 256] = part.reshape(16, 8, 256).astype(BF)
     to_all(lambda r: filt(4, r, dw1.at[peer(r)], dw1_in.at[f]).start())
     two_sums.reduce()
 
     def get_one(r, total):
         filt(4, r, dw1.at[peer(r)], dw1_in.at[source(r)]).wait_recv()
-        return total + dw1_in[source(r)]
-
-    first = from_all(get_one, dw1[f])
+        return total + dw1_in[source(r)].astype(F32)
+
+    first = from_all(get_one, dw1[f].astype(F32))
     for j in range(W1_BLOCKS):
         one[j] = first[:, j * 128 : (j + 1) * 128]
     one_first = TAPS if slabs >= TAPS + W1_BLOCKS else 0
@@ -403,6 +417,7 @@
     one_sums.reduce()
     two_sums.finish()
     one_sums.finish()
+    store.wait()
 
 
 def owners(blocks, n):
@@ -423,12 +438,14 @@
         ((2, 2, 4, 8, 128), BF), ((2, 4, 8, 128), BF), ((2, 4, 8, 128), BF),
         ((3, 2, 4, 6, 8, 128), F32), ((2, 2, 4, 216, 128), F32),
         ((16, 128, 128), BF), ((16, 128, 128), BF),
-        ((16, 8, 512), F32), ((16, 8, 512), F32), ((128, 216), BF), ((128, 128), F32),
+        ((16, 8, 512), BF), ((16, 8, 512), BF), ((128, 216), BF), ((128, 128), F32),
         ((two_size, 8, 128), F32), ((slabs, two_count[1], 8, 128), F32),
         ((two_count[1], 8, 128), F32),
         ((one_size, 8, 128), F32), ((slabs, one_count[1], 8, 128), F32),
         ((one_count[1], 8, 128), F32),
         ((2, 2, 4, 8, 128), F32), ((2, 2, 4, 8, 128), F32),
+        ((256, 256), BF), ((216, 128), BF), ((2, 8, 2, 4, 128), BF),
+        ((2, 8, 2, 4, 128), BF),
     ]
     return pl.pallas_call(
         functools.partial(level_kernel, filts, slabs, two_count, one_count),
@@ -437,11 +454,11 @@
             jax.ShapeDtypeStruct((two_size, 8, 128), F32),
             jax.ShapeDtypeStruct((one_size, 8, 128), F32),
         ],
-        in_specs=[VMEM] * 4,
-        out_specs=[VMEM] * 3,
+        in_specs=[ANY, VMEM, ANY, ANY],
+        out_specs=[ANY, VMEM, VMEM],
         scratch_shapes=[pltpu.VMEM(shape, dtype) for shape, dtype in buffers]
         + [
-            sem((5, filts)), sem((5, filts)), sem((4,)), sem((4,)),
+            sem((4,)), sem((5, filts)), sem((5, filts)), sem((4,)), sem((4,)),
             sem((two_count[0],)), sem((slabs,)), sem((slabs,)), sem((two_count[0],)),
             sem((one_count[0],)), sem((slabs,)), sem((slabs,)), sem((one_count[0],)),
         ],

time: 96.1 us -> 93.4 us (0.972)
  Pallas kernels: 90.6 us -> 87.9 us
    pallas_call x1, Pallas kernels: 90.6 us -> 87.9 us  [level(): pl.pallas_call(functools.partial(level_kernel, filts, slabs, two_count, o...]
where the time goes in v5:
time: 93.4 us; the launch traced here: 93 us
  Pallas kernels  87.9 us (94%)
  local copies, waits for them, and re-layouts  4.46 us (5%)
    pallas_call x1, Pallas kernels, level(): pl.pallas_call(functools.partial(level_kernel, filts, slabs, two_count, o...  87.9 us
    unnamed x7, local copies, waits for them, and re-layouts  2.07 us

profile of v5, /device:TPU:1, one launch (start us, length us, event | category | flops | bytes accessed | tf_op | source)
XLA Modules:
  0.0 93.0 jit_solution(10129013171457688998)
XLA Ops:
  0.6 0.9 copy.9
  1.5 0.7 copy.10.w1_ref
  2.2 87.9 %level.1 = (bf16[2,8,2,4,128]{4,3,2,1,0:T(4,128)(2,1)}, f32[27,8,128]{2,1,0:T(8,128)}, f32[4,8,128]{2,1,0:T(8,128)}) custom-call(bf16[256,256]{1,0:T(8,128)(2,1)} %bitcast.16, bf16[8,512]{1,0:T(8,128)(2,1)} %copy.10.w1_ref, bf16[216,128]{1,0:T(8,128)(2,1)} %bitcast.18, bf16[2,8,2,4,128]{4,3,2,1,0:T(4,128)(2,1)} %og_hbm.1), custom_call_target="tpu_custom_call" | custom-call | tf_op jit(solution)/shard_map/level/pallas_call | solution.py:450
  90.1 0.8 copy.11
  91.0 0.0 copy-start.1
  91.0 0.0 copy-start
  91.0 0.8 copy.12
  91.8 0.0 copy-done.1
  91.8 0.6 copy.15
  92.4 0.0 copy-done
  92.4 0.6 copy.16
Async XLA Ops:
  91.0 0.8 copy-start.1
  91.0 1.4 %copy-start = (f32[27,8,128]{2,1,0:T(8,128)S(1)}, f32[27,8,128]{2,1,0:T(8,128)}, u32[]{:S(2)}) copy-start(f32[27,8,128]{2,1,0:T(8,128)} %get-tuple-element.8) | copy-start | bytes 331780

commit v6 on v5

--- a/solution.py
+++ b/solution.py
@@ -166,12 +166,12 @@
 
 def level_kernel(
     filts, slabs, two_count, one_count,
-    x_hbm, w1_ref, w2_hbm, og_hbm,
-    result_hbm, two_out, one_out,
+    x_hbm, w1_raw, w2_hbm, og_hbm,
+    result_hbm, two_out, w1_out,
     piece, x_all, w_all, hid, y, own, up, down, below, above,
     sg, sg_below, sg_above, view, s, mid, mid_in, dw1, dw1_in, w2_t, pre_ref,
     two, two_in, two_sum, one, one_in, one_sum,
-    og, res, x_ref, w2_ref, og_ref, result_ref, ls, fs, fr, hs, hr, ts_a, tr_a, ts_b, tr_b, os_a, or_a, os_b, or_b,
+    og, res, w1_ref, w1_wide, order, x_perm, one_out, x_ref, w2_ref, og_ref, result_ref, ls, fs, fr, hs, hr, ts_a, tr_a, ts_b, tr_b, os_a, or_a, os_b, or_b,
 ):
     f, z = lax.axis_index("filt"), lax.axis_index("slab")
     barrier = pltpu.get_barrier_semaphore()
@@ -227,6 +227,13 @@
     cut = jnp.dot(half, columns, preferred_element_type=F32).astype(BF)
     piece[...] = cut.reshape(piece.shape)
     x_all[f] = piece[f]
+    for n in range(8):
+        for t in range(4):
+            both = w1_raw[n, t].astype(F32)
+            for k in range(2):
+                w1_wide[k * 4 + t, n : n + 1, :] = both[k : k + 1, :]
+    for t in range(8):
+        w1_ref[:, t * 64 : (t + 1) * 64] = w1_wide[t].astype(BF)
     w_all[f] = w1_ref[...]
     pl.semaphore_wait(barrier, filts + slabs - 2)
 
@@ -235,6 +242,7 @@
         filt(1, r, w1_ref, w_all.at[f]).start()
 
     to_all(send_x)
+    order[...] = one_hot(lambda o: ((o & 63) << 2) + (o >> 6), 256)
     loads[1].wait()
     loads[2].wait()
     for b in range(2):
@@ -254,6 +262,8 @@
 
     to_all(get_x)
     x = x_all[...].reshape(256, 256)
+    x = jnp.dot(order[...], x, preferred_element_type=F32).astype(BF)
+    x_perm[...] = x
     w = w_all[...].reshape(128, 512)
     pre = jnp.dot(w[:, :256], x[:, :128], preferred_element_type=F32)
     pre += jnp.dot(w[:, 256:], x[:, 128:], preferred_element_type=F32)
@@ -383,7 +393,7 @@
 
     mid_grad = from_all(get_mid, mid[f].astype(F32))
     grad = (mid_grad * silu_slope(pre_ref[...])).astype(BF)
-    x = x_all[...].reshape(256, 256)
+    x = x_perm[...]
     for k in range(2):
         part = nt_dot(grad, x[:, k * 128 : (k + 1) * 128])
         dw1[:, :, k * 256 : (k + 1) * 256] = part.reshape(16, 8, 256).astype(BF)
@@ -417,6 +427,9 @@
     one_sums.reduce()
     two_sums.finish()
     one_sums.finish()
+    for j in range(W1_BLOCKS):
+        for t in range(2):
+            w1_out[:, j % 2 * 2 + t, j // 2, :] = one_out[j][:, t * 64 : (t + 1) * 64]
     store.wait()
 
 
@@ -444,6 +457,8 @@
         ((one_size, 8, 128), F32), ((slabs, one_count[1], 8, 128), F32),
         ((one_count[1], 8, 128), F32),
         ((2, 2, 4, 8, 128), F32), ((2, 2, 4, 8, 128), F32),
+        ((8, 512), BF), ((8, 8, 64), F32), ((256, 256), BF), ((256, 256), BF),
+        ((one_size, 8, 128), F32),
         ((256, 256), BF), ((216, 128), BF), ((2, 8, 2, 4, 128), BF),
         ((2, 8, 2, 4, 128), BF),
     ]
@@ -452,7 +467,7 @@
         out_shape=[
             jax.ShapeDtypeStruct((2, 8, 2, 4, 128), BF),
             jax.ShapeDtypeStruct((two_size, 8, 128), F32),
-            jax.ShapeDtypeStruct((one_size, 8, 128), F32),
+            jax.ShapeDtypeStruct((8, 4, 2, 64), F32),
         ],
         in_specs=[ANY, VMEM, ANY, ANY],
         out_specs=[ANY, VMEM, VMEM],
@@ -468,12 +483,11 @@
 
 
 def on_device(volume, first_weight, second_weight, out_grad):
-    w1 = first_weight.transpose(1, 4, 0, 2, 3).reshape(8, 512)
+    w1 = first_weight.transpose(1, 2, 3, 4, 0).reshape(8, 4, 2, 64)
     w2 = second_weight.transpose(2, 3, 4, 1, 0).reshape(216, 128)
     result, two, one = level(volume.reshape(256, 256), w1, w2, out_grad)
     weight_two = two[:TAPS].reshape(3, 3, 3, 8, 128).transpose(4, 3, 0, 1, 2)
-    one = one.reshape(2, 2, 8, 32, 2, 2).transpose(1, 3, 2, 4, 5, 0)
-    weight_one = one.reshape(64, 8, 2, 2, 2)
+    weight_one = one.reshape(8, 2, 2, 2, 64).transpose(4, 0, 1, 2, 3)
     return (result, weight_one, weight_two)
 
 

time: 93.4 us -> 92 us (0.985)
  local copies, waits for them, and re-layouts: 4.46 us -> 3.44 us
    unnamed x7 -> x5, local copies, waits for them, and re-layouts: 2.07 us -> 3.44 us
where the time goes in v6:
time: 92 us; the launch traced here: 91.7 us
  Pallas kernels  87.6 us (95%)
  local copies, waits for them, and re-layouts  3.44 us (4%)
    pallas_call x1, Pallas kernels, level(): pl.pallas_call(functools.partial(level_kernel, filts, slabs, two_count, o...  87.6 us
    unnamed x5, local copies, waits for them, and re-layouts  3.44 us

profile of v6, /device:TPU:1, one launch (start us, length us, event | category | flops | bytes accessed | tf_op | source)
XLA Modules:
  0.0 91.7 jit_solution(10966450196416424857)
XLA Ops:
  0.6 87.6 %level.1 = (bf16[2,8,2,4,128]{4,3,2,1,0:T(4,128)(2,1)}, f32[27,8,128]{2,1,0:T(8,128)}, f32[8,4,2,64]{3,2,1,0:T(2,128)}) custom-call(bf16[256,256]{1,0:T(8,128)(2,1)} %bitcast.13, bf16[8,4,2,64]{3,2,1,0:T(2,128)(2,1)} %bitcast.17, bf16[216,128]{1,0:T(8,128)(2,1)} %bitcast.15, bf16[2,8,2,4,128]{4,3,2,1,0:T(4,128)(2,1)} %og_hbm.1), custom_call_target="tpu_custom_call" | custom-call | tf_op jit(solution)/shard_map/level/pallas_call | solution.py:465
  88.3 0.0 copy-start
  88.3 1.4 %copy.10 = bf16[2,8,2,4,128]{4,3,2,1,0:T(4,128)(2,1)} copy(bf16[2,8,2,4,128]{4,3,2,1,0:T(4,128)(2,1)} %get-tuple-element.12) | data formatting | bytes 65536
  89.7 1.4 %copy.11 = f32[64,8,2,2,2]{0,4,3,2,1:T(2,128)} copy(f32[64,8,2,2,2]{0,4,3,2,1:T(2,128)} %bitcast.16) | data formatting | bytes 32768
  91.1 0.0 copy-done
  91.1 0.6 copy.12
Async XLA Ops:
  88.3 2.8 %copy-start = (f32[27,8,128]{2,1,0:T(8,128)S(1)}, f32[27,8,128]{2,1,0:T(8,128)}, u32[]{:S(2)}) copy-start(f32[27,8,128]{2,1,0:T(8,128)} %get-tuple-element.8) | copy-start | bytes 331780

commit v7 on v6

--- a/solution.py
+++ b/solution.py
@@ -282,7 +282,7 @@
         spread(source(r))
 
     from_all(lambda r, carry: (get_hidden(r), carry)[1], 0)
-    for d in (-1, 2, 0, 1):
+    def stencil(d):
         total = None
         for g in range(3):
             part = None
@@ -303,6 +303,8 @@
         else:
             own[d] = total
 
+    stencil(-1)
+    stencil(2)
     after, before = lax.rem(z + 1, slabs), lax.rem(z + slabs - 1, slabs)
 
     def rims(i, block_up, block_down, from_below, from_above):
@@ -314,6 +316,8 @@
     first_rims = rims(0, up, down, below, above)
     for copy in first_rims:
         copy.start()
+    stencil(0)
+    stencil(1)
     inside = (z > 0, z < slabs - 1)
     for copy in first_rims:
         copy.wait_recv()

time: 92 us -> 92 us (level)
  no operation moved by 1% of the time
where the time goes in v7:
time: 92 us; the launch traced here: 91.7 us
  Pallas kernels  87.6 us (95%)
  local copies, waits for them, and re-layouts  3.44 us (4%)
    pallas_call x1, Pallas kernels, level(): pl.pallas_call(functools.partial(level_kernel, filts, slabs, two_count, o...  87.6 us
    unnamed x5, local copies, waits for them, and re-layouts  3.44 us

profile of v7, /device:TPU:1, one launch (start us, length us, event | category | flops | bytes accessed | tf_op | source)
XLA Modules:
  0.0 91.7 jit_solution(14452683492817370912)
XLA Ops:
  0.6 87.6 %level.1 = (bf16[2,8,2,4,128]{4,3,2,1,0:T(4,128)(2,1)}, f32[27,8,128]{2,1,0:T(8,128)}, f32[8,4,2,64]{3,2,1,0:T(2,128)}) custom-call(bf16[256,256]{1,0:T(8,128)(2,1)} %bitcast.13, bf16[8,4,2,64]{3,2,1,0:T(2,128)(2,1)} %bitcast.17, bf16[216,128]{1,0:T(8,128)(2,1)} %bitcast.15, bf16[2,8,2,4,128]{4,3,2,1,0:T(4,128)(2,1)} %og_hbm.1), custom_call_target="tpu_custom_call" | custom-call | tf_op jit(solution)/shard_map/level/pallas_call | solution.py:469
  88.2 0.0 copy-start
  88.2 1.4 %copy.10 = bf16[2,8,2,4,128]{4,3,2,1,0:T(4,128)(2,1)} copy(bf16[2,8,2,4,128]{4,3,2,1,0:T(4,128)(2,1)} %get-tuple-element.12) | data formatting | bytes 65536
  89.7 1.4 %copy.11 = f32[64,8,2,2,2]{0,4,3,2,1:T(2,128)} copy(f32[64,8,2,2,2]{0,4,3,2,1:T(2,128)} %bitcast.16) | data formatting | bytes 32768
  91.0 0.0 copy-done
  91.0 0.6 copy.12
Async XLA Ops:
  88.2 2.8 %copy-start = (f32[27,8,128]{2,1,0:T(8,128)S(1)}, f32[27,8,128]{2,1,0:T(8,128)}, u32[]{:S(2)}) copy-start(f32[27,8,128]{2,1,0:T(8,128)} %get-tuple-element.8) | copy-start | bytes 331780
